TPU v7x, 32 devices: a whole 2x2x4 slice. The times are simulated.
32 devices in a mesh: orb: 8 (over z, x), cell: 4 (over y, core).
Axes of the slice: x: 2, y: 2, z: 4, core: 2. Of those that a mesh axis runs over, the one named last changes fastest.
Arguments:
- potentials: bfloat16 [96, 65536], P(None, 'cell'), may hold values from -6 to 6
- orbitals: bfloat16 [512, 65536], P('orb', 'cell'), may hold values from -6 to 6
- levels: float32 [512], replicated, may hold values from 0.2 to 4
- occ_index: int32 [64], replicated, may hold values from 0 to 511, as said below
- coul_rows: float32 [256, 256], replicated, may hold values from -0.375 to 0.375
- coul_cols: float32 [256, 256], replicated, may hold values from -0.375 to 0.375
Outputs:
- screened: float32 [96, 256, 256], P('orb', 'cell')
Inputs may be any that keep to these rules, and one draw needn't show every extreme that they name: `occ_index`: 64 distinct orbital numbers.
All inputs are finite; a program needn't handle non-finite values.
Results may differ from a plain program's by a relative error of at most 0.004.
Values may be sent and summed in bfloat16 or wider, within the bound.
A program may use at most 128 MiB of HBM per device.

v0:
```python
import jax
import jax.numpy as jnp
from jax import lax
from jax.sharding import PartitionSpec as P

SIDE = 256


def pair_block(occ_block, basis):
    joined = occ_block.astype(jnp.float32)[:, None, :] * basis.astype(jnp.float32)[None, :, :]
    return joined.reshape(-1, basis.shape[1]).astype(jnp.bfloat16)


def body(potentials, orbitals, levels, occ_index, coul_rows, coul_cols):
    points_dev = orbitals.shape[1]
    volume = points_dev * lax.axis_size("cell")
    orb_count = lax.axis_size("orb")
    my_rank = lax.axis_index("orb")
    per_orb = orbitals.shape[0]
    labels = jnp.arange(levels.shape[0], dtype=jnp.int32)
    marked = jnp.any(occ_index[:, None] == labels[None, :], axis=0)
    empty_all = 1.0 - marked.astype(jnp.float32)
    slot_count = occ_index.shape[0] // orb_count
    owned_ids = my_rank * per_orb + jnp.arange(per_orb, dtype=jnp.int32)
    picker = (occ_index[:, None] == owned_ids[None, :]).astype(jnp.bfloat16)
    picked = jnp.dot(picker, orbitals, preferred_element_type=jnp.float32).astype(jnp.bfloat16)
    gathered = lax.psum(picked, "orb").astype(jnp.float32).astype(jnp.bfloat16)
    occ_rows = gathered.reshape(slot_count, orb_count, points_dev)
    occ_level = levels[occ_index].reshape(slot_count, orb_count)
    basis_level = lax.dynamic_slice_in_dim(levels, my_rank * per_orb, per_orb)
    basis_empty = lax.dynamic_slice_in_dim(empty_all, my_rank * per_orb, per_orb)
    weights = (
        -2.0 * basis_empty[None, None, :] / (occ_level[:, :, None] + basis_level[None, None, :])
    )
    weights = (weights / volume).reshape(slot_count, -1)

    def intersection_step(unused_carry, occ_block):
        products = pair_block(occ_block, orbitals)
        partial_value = lax.dot_general(
            products, potentials, (((1,), (1,)), ((), ())), preferred_element_type=jnp.float32
        )
        return (unused_carry, partial_value)

    _, intersections = lax.scan(intersection_step, jnp.zeros((), jnp.float32), occ_rows)
    intersections = lax.psum(intersections, "cell")
    guesses = (intersections * weights[:, :, None]).astype(jnp.bfloat16)

    def response_step(running, pieces):
        occ_block, guess_block = pieces
        products = pair_block(occ_block, orbitals)
        running = running + lax.dot_general(
            guess_block, products, (((0,), (0,)), ((), ())), preferred_element_type=jnp.float32
        )
        return (running, None)

    response, _ = lax.scan(
        response_step,
        jnp.zeros((potentials.shape[0], points_dev), jnp.float32),
        (occ_rows, guesses),
    )
    owned_sum = lax.psum_scatter(response, "orb", scatter_dimension=0, tiled=True)
    row_count = points_dev // SIDE
    plane_rows = owned_sum.reshape(owned_sum.shape[0], row_count, SIDE)
    by_columns = jnp.einsum("vrc,dc->vrd", plane_rows, coul_cols, precision=lax.Precision.HIGHEST)
    mixed_rows = jnp.einsum(
        "ab,vbc->vac",
        coul_rows,
        lax.all_to_all(by_columns, "cell", split_axis=2, concat_axis=1, tiled=True),
        precision=lax.Precision.HIGHEST,
    )
    return lax.all_to_all(mixed_rows, "cell", split_axis=1, concat_axis=2, tiled=True)


def solution(mesh):
    placed = (P(None, "cell"), P("orb", "cell"), P(), P(), P(), P())
    return jax.shard_map(
        body, mesh=mesh, in_specs=placed, out_specs=P("orb", "cell", None), check_vma=False
    )
```

profile of v0, /device:TPU:10, one launch (start us, length us, event | category | flops | bytes accessed | tf_op | source)
XLA Modules:
  0.0 713.9 jit_solution(4356160588785237117)
XLA Ops:
  6.6 3.9 fusion.5
  10.6 103.4 %all-reduce.5.cloned.1.call-done = bf16[8,8,16384]{2,1,0:T(8,128)(2,1)} async-done(((bf16[8,8,16384]{2,1,0:T(8,128)(2,1)}), bf16[8,8,16384]{2,1,0:T(8,128)(2,1)}) %all-reduce.5.cloned.1.call-update) | async-done | bytes 2097168 | tf_op jit(solution)/shard_map/psum | solution.py:27
  114.1 82.7 %while.21 = (s32[]{:T(128)}, f32[8,512,96]{1,2,0:T(8,128)}, bf16[8,8,16384]{2,1,0:T(8,128)(2,1)}, bf16[64,16384]{1,0:T(8,128)(2,1)S(1)}, bf16[96,16384]{1,0:T(8,128)(2,1)}, /*index=5*/s32[]{:T(128)}) while((s32[]{:T(128)}, f32[8,512,96]{1,2,0:T(8,128)}, bf16[8,8,16384]{2,1,0:T(8,128)(2,1)}, bf16[64,16384]{1,0:T(8,128)(2,1)S(1)}, ...), condition=%wide.region_2.3_spmd, body=%wide.region_1.0_spmd.sunk | while | flops 1628569600 | bytes 61276772 | solution.py:44
  115.4 3.1 multiply_convert_fusion.5
  118.4 6.0 fusion.26
  125.7 3.1 multiply_convert_fusion.5
  128.8 6.0 fusion.26
  136.0 3.1 multiply_convert_fusion.5
  139.1 6.0 fusion.26
  146.4 3.1 multiply_convert_fusion.5
  149.4 6.0 fusion.26
  156.7 3.1 multiply_convert_fusion.5
  159.8 6.0 fusion.26
  167.0 3.1 multiply_convert_fusion.5
  170.1 6.0 fusion.26
  177.4 3.1 multiply_convert_fusion.5
  180.5 6.0 fusion.26
  187.7 3.1 multiply_convert_fusion.5
  190.8 6.0 fusion.26
  196.7 2.9 copy.18
  201.0 49.9 %all-reduce.7.cloned.1.call-done = f32[8,512,96]{2,1,0:T(8,128)} async-done(((f32[8,512,96]{2,1,0:T(8,128)}), f32[8,512,96]{2,1,0:T(8,128)}) %all-reduce.7.cloned.1.call-update) | async-done | bytes 1572880 | tf_op jit(solution)/shard_map/psum | solution.py:45
  252.8 163.5 %while.22 = (s32[]{:T(128)}, f32[96,16384]{1,0:T(8,128)}, bf16[8,512,96]{2,1,0:T(8,128)(2,1)S(1)}, bf16[8,8,16384]{2,1,0:T(8,128)(2,1)}, bf16[64,16384]{1,0:T(8,128)(2,1)S(1)}, /*index=5*/s32[]{:T(128)}, s32[]{:T(128)}) while((s32[]{:T(128)}, f32[96,16384]{1,0:T(8,128)}, bf16[8,512,96]{2,1,0:T(8,128)(2,1)S(1)}, ...), condition=%wide.region_6.7_spmd.clone, body=%wide.region_5.6_spmd.clone.sunk | while | flops 1631715328 | bytes 58064988 | solution.py:56
  254.1 6.1 multiply_convert_fusion.6
  260.2 11.5 %convolution_add_fusion.2 = f32[96,16384]{1,0:T(8,128)} fusion(bf16[512,16384]{1,0:T(8,128)(2,1)} %bitcast.67, f32[96,16384]{1,0:T(8,128)} %get-tuple-element.187, pred[]{:T(512)S(6)} %compare.3, bf16[8,512,96]{2,1,0:T(8,128)(2,1)S(1)} %get-tuple-element.195, s32[]{:T(128)} %get-tuple-element.186), kind=kOutput, calls=%fused_computation.6.clone.1 | convolution fusion | flops 1613758464 | bytes 29491204 | tf_op jit(solution)/shard_map/while/body/eval_jaxpr/dot_general | solution.py:51
  273.0 6.1 multiply_convert_fusion.6
  279.1 13.3 %convolution_add_fusion.2 = f32[96,16384]{1,0:T(8,128)} fusion(bf16[512,16384]{1,0:T(8,128)(2,1)} %bitcast.67, f32[96,16384]{1,0:T(8,128)} %get-tuple-element.187, pred[]{:T(512)S(6)} %compare.3, bf16[8,512,96]{2,1,0:T(8,128)(2,1)S(1)} %get-tuple-element.195, s32[]{:T(128)} %get-tuple-element.186), kind=kOutput, calls=%fused_computation.6.clone.1 | convolution fusion | flops 1613758464 | bytes 29491204 | tf_op jit(solution)/shard_map/while/body/eval_jaxpr/dot_general | solution.py:51
  293.6 6.1 multiply_convert_fusion.6
  299.7 13.3 %convolution_add_fusion.2 = f32[96,16384]{1,0:T(8,128)} fusion(bf16[512,16384]{1,0:T(8,128)(2,1)} %bitcast.67, f32[96,16384]{1,0:T(8,128)} %get-tuple-element.187, pred[]{:T(512)S(6)} %compare.3, bf16[8,512,96]{2,1,0:T(8,128)(2,1)S(1)} %get-tuple-element.195, s32[]{:T(128)} %get-tuple-element.186), kind=kOutput, calls=%fused_computation.6.clone.1 | convolution fusion | flops 1613758464 | bytes 29491204 | tf_op jit(solution)/shard_map/while/body/eval_jaxpr/dot_general | solution.py:51
  314.3 6.1 multiply_convert_fusion.6
  320.4 13.3 %convolution_add_fusion.2 = f32[96,16384]{1,0:T(8,128)} fusion(bf16[512,16384]{1,0:T(8,128)(2,1)} %bitcast.67, f32[96,16384]{1,0:T(8,128)} %get-tuple-element.187, pred[]{:T(512)S(6)} %compare.3, bf16[8,512,96]{2,1,0:T(8,128)(2,1)S(1)} %get-tuple-element.195, s32[]{:T(128)} %get-tuple-element.186), kind=kOutput, calls=%fused_computation.6.clone.1 | convolution fusion | flops 1613758464 | bytes 29491204 | tf_op jit(solution)/shard_map/while/body/eval_jaxpr/dot_general | solution.py:51
  335.0 6.1 multiply_convert_fusion.6
  341.1 13.3 %convolution_add_fusion.2 = f32[96,16384]{1,0:T(8,128)} fusion(bf16[512,16384]{1,0:T(8,128)(2,1)} %bitcast.67, f32[96,16384]{1,0:T(8,128)} %get-tuple-element.187, pred[]{:T(512)S(6)} %compare.3, bf16[8,512,96]{2,1,0:T(8,128)(2,1)S(1)} %get-tuple-element.195, s32[]{:T(128)} %get-tuple-element.186), kind=kOutput, calls=%fused_computation.6.clone.1 | convolution fusion | flops 1613758464 | bytes 29491204 | tf_op jit(solution)/shard_map/while/body/eval_jaxpr/dot_general | solution.py:51
  355.6 6.1 multiply_convert_fusion.6
  361.7 13.3 %convolution_add_fusion.2 = f32[96,16384]{1,0:T(8,128)} fusion(bf16[512,16384]{1,0:T(8,128)(2,1)} %bitcast.67, f32[96,16384]{1,0:T(8,128)} %get-tuple-element.187, pred[]{:T(512)S(6)} %compare.3, bf16[8,512,96]{2,1,0:T(8,128)(2,1)S(1)} %get-tuple-element.195, s32[]{:T(128)} %get-tuple-element.186), kind=kOutput, calls=%fused_computation.6.clone.1 | convolution fusion | flops 1613758464 | bytes 29491204 | tf_op jit(solution)/shard_map/while/body/eval_jaxpr/dot_general | solution.py:51
  376.3 6.1 multiply_convert_fusion.6
  382.4 13.3 %convolution_add_fusion.2 = f32[96,16384]{1,0:T(8,128)} fusion(bf16[512,16384]{1,0:T(8,128)(2,1)} %bitcast.67, f32[96,16384]{1,0:T(8,128)} %get-tuple-element.187, pred[]{:T(512)S(6)} %compare.3, bf16[8,512,96]{2,1,0:T(8,128)(2,1)S(1)} %get-tuple-element.195, s32[]{:T(128)} %get-tuple-element.186), kind=kOutput, calls=%fused_computation.6.clone.1 | convolution fusion | flops 1613758464 | bytes 29491204 | tf_op jit(solution)/shard_map/while/body/eval_jaxpr/dot_general | solution.py:51
  396.9 6.1 multiply_convert_fusion.6
  403.0 13.3 %convolution_add_fusion.2 = f32[96,16384]{1,0:T(8,128)} fusion(bf16[512,16384]{1,0:T(8,128)(2,1)} %bitcast.67, f32[96,16384]{1,0:T(8,128)} %get-tuple-element.187, pred[]{:T(512)S(6)} %compare.3, bf16[8,512,96]{2,1,0:T(8,128)(2,1)S(1)} %get-tuple-element.195, s32[]{:T(128)} %get-tuple-element.186), kind=kOutput, calls=%fused_computation.6.clone.1 | convolution fusion | flops 1613758464 | bytes 29491204 | tf_op jit(solution)/shard_map/while/body/eval_jaxpr/dot_general | solution.py:51
  416.3 171.2 %fusion = f32[16,16384]{1,0:T(8,128)S(1)} fusion(f32[96,16384]{1,0:T(8,128)} %get-tuple-element.60), kind=kCustom, calls=%all-reduce-scatter | all-reduce-scatter fusion | flops 2097153 | bytes 7340544
  587.5 2.2 collective-permute-start
  593.2 41.8 %collective-permute-done.1 = f32[12,16384]{1,0:T(8,128)} collective-permute-done((f32[12,16384]{1,0:T(8,128)S(1)}, f32[12,16384]{1,0:T(8,128)}, u32[]{:S(2)}, u32[]{:S(2)}) %collective-permute-start.1) | collective-permute-done | bytes 786464
  635.1 18.2 %concatenate = f32[44,16384]{1,0:T(8,128)} concatenate(f32[12,16384]{1,0:T(8,128)} %collective-permute-done.1, f32[16,16384]{1,0:T(8,128)S(1)} %collective-permute-done, f32[16,16384]{1,0:T(8,128)S(1)} %fusion), dimensions={0} | concatenate | bytes 5767168
  658.3 14.0 %all_to_all.36 = f32[4,1,49152]{2,1,0:T(1,128)S(1)} all-to-all(f32[4,1,49152]{2,1,0:T(1,128)S(1)} %reshape.93), channel_id=1, replica_groups=mesh['orb'=8,'cell'=4] {'cell'}, dimensions={0} | all-to-all | bytes 1572864 | tf_op jit(solution)/shard_map/all_to_all | solution.py:68
  672.9 2.9 reduce
  678.8 2.2 all_to_all.29
  684.2 14.0 %all_to_all.37 = f32[4,1,49152]{2,1,0:T(1,128)S(1)} all-to-all(f32[4,1,49152]{2,1,0:T(1,128)S(1)} %reshape.95), channel_id=1, replica_groups=mesh['orb'=8,'cell'=4] {'cell'}, dimensions={0} | all-to-all | bytes 1572864 | tf_op jit(solution)/shard_map/all_to_all | solution.py:71
  698.3 2.9 reduce.1
  704.2 3.0 all_to_all.33
  (100 shorter events, 41.1 us)
Async XLA Ops:
  6.5 648.6 %copy-start = (f32[256,256]{1,0:T(8,128)S(1)}, f32[256,256]{1,0:T(8,128)}, u32[]{:S(2)}) copy-start(f32[256,256]{1,0:T(8,128)} %param.15) | copy-start | bytes 786436
  6.5 4.0 copy-start.5
  6.5 107.5 %copy-start.1 = (bf16[64,16384]{1,0:T(8,128)(2,1)S(1)}, bf16[64,16384]{1,0:T(8,128)(2,1)}, u32[]{:S(2)}) copy-start(bf16[64,16384]{1,0:T(8,128)(2,1)} %param.11) | copy-start | bytes 6291460
  6.5 107.5 %all-reduce.5.cloned.1.call-start = ((), (), s32[]{:S(2)}) async-start(), calls=%async_computation.2 | async-start | bytes 4194304 | tf_op jit(solution)/shard_map/psum | solution.py:27
  10.5 240.4 %all-reduce.7.cloned.1.call-start = ((), (), s32[]{:S(2)}) async-start(), calls=%async_computation.3 | async-start | bytes 4194304 | tf_op jit(solution)/shard_map/psum | solution.py:45
  115.3 3.1 copy-start.3
  125.7 3.1 copy-start.3
  136.0 3.1 copy-start.3
  146.3 3.1 copy-start.3
  156.7 3.1 copy-start.3
  167.0 3.1 copy-start.3
  177.4 3.1 copy-start.3
  187.7 3.1 copy-start.3
  196.7 3.1 copy-start.2
  416.3 175.7 %copy-start.6 = (u32[32]{0:T(128)S(1)}, u32[32]{0:T(128)}, u32[]{:S(2)}) copy-start(u32[32]{0:T(128)} %constant.45) | copy-start | bytes 388
  587.5 47.5 %collective-permute-start = (f32[16,16384]{1,0:T(8,128)S(1)}, f32[16,16384]{1,0:T(8,128)S(1)}, u32[]{:S(2)}, u32[]{:S(2)}) collective-permute-start(f32[16,16384]{1,0:T(8,128)S(1)} %fusion), channel_id=1, source_target_pairs={{0,4},{4,8},{8,12},{12,16},{16,20},{20,24},{24,28},{1,5},{5,9},{9,... | collective-permute-start | bytes 3145736
  589.9 45.2 %collective-permute-start.1 = (f32[12,16384]{1,0:T(8,128)S(1)}, f32[12,16384]{1,0:T(8,128)}, u32[]{:S(2)}, u32[]{:S(2)}) collective-permute-start(f32[12,16384]{1,0:T(8,128)S(1)} %slice.2), channel_id=1, source_target_pairs={{0,8},{4,12},{8,16},{12,20},{16,24},{20,28},{1,9},{5,13},{9,17},{1... | collective-permute-start | bytes 2359304
  675.8 5.2 copy-start.4
Sparse Core Ops, SparseCore 0:
  11.0 103.0 all-reduce.4
  199.8 51.0 all-reduce.6
where the time goes:
time: 715 us; the launch traced here: 714 us
  blocking collectives  199 us (28%)
  waiting for transfers between devices  195 us (27%)
  matrix products  158 us (22%)
  other arithmetic  101 us (14%)
  local copies, waits for them, and re-layouts  41.3 us (6%)
  between operations  14.3 us (2%)
    unnamed x1, blocking collectives  171 us
    dot_general x8, matrix products, response_step(): lax.dot_general(guess_block, products, (((0,), (0,)), ((), ())), preferre...  105 us
    psum x1, waiting for transfers between devices, body(): gathered = lax.psum(picked, 'orb').astype(jnp.float32).astype(jnp.bfloat16)  103 us
    convert_element_type x16, other arithmetic, pair_block(): return joined.reshape(-1, basis.shape[1]).astype(jnp.bfloat16)  73.3 us
    psum x1, waiting for transfers between devices, body(): intersections = lax.psum(intersections, 'cell')  49.9 us
    dot_general x8, matrix products, intersection_step(): lax.dot_general(products, potentials, (((1,), (1,)), ((), ())), preferred...  47.8 us
    unnamed x4, waiting for transfers between devices  41.9 us
    unnamed x21, local copies, waits for them, and re-layouts  24.4 us
  transfers between devices with their start and end apart: 4, of which 3 were waited for; matrix products, arithmetic and copies ran while one was open for 0% of the time, Pallas kernels for 0%

commit v1 on v0

v1 whole, which is shorter than its diff:
```python
import functools

import jax
import jax.numpy as jnp
import numpy as np
from jax import lax
from jax.experimental import pallas as pl
from jax.experimental.pallas import tpu as pltpu
from jax.sharding import PartitionSpec as P

SIDE = 256
GATHER_CHUNKS = 2
RESPONSE_CHUNKS = 4
VMEM = 56 * 1024 * 1024


def swap(x, axis, bit):
    n = lax.axis_size(axis)
    return lax.ppermute(x, axis, [(s, s ^ bit) for s in range(n)])


def upper(axis, bit):
    return (lax.axis_index(axis) // bit) % 2


def halve(x, axis, bit, dim, wire=None):
    half = x.shape[dim] // 2
    side = upper(axis, bit)
    keep = lax.dynamic_slice_in_dim(x, side * half, half, dim)
    send = lax.dynamic_slice_in_dim(x, (1 - side) * half, half, dim)
    if wire is not None:
        send = send.astype(wire)
    return keep + swap(send, axis, bit).astype(x.dtype)


def double(x, axis, bit, dim):
    other = swap(x, axis, bit)
    low = upper(axis, bit) == 0
    return jnp.concatenate([jnp.where(low, x, other), jnp.where(low, other, x)], dim)


def bits_of(axis):
    n = lax.axis_size(axis)
    return [1 << k for k in range(n.bit_length() - 1)]


def pair_rows(occ_ref, orb, first, count):
    return jnp.concatenate([occ_ref[i : i + 1, :] * orb for i in range(first, first + count)], 0)


def project_kernel(group, occ_ref, orb_ref, pot_ref, out_ref, acc):
    step = pl.program_id(0)

    @pl.when(step == 0)
    def _():
        acc[...] = jnp.zeros_like(acc)

    turned = pot_ref[...].T
    orb = orb_ref[...]
    rows = group * orb.shape[0]
    for k in range(occ_ref.shape[0] // group):
        pairs = pair_rows(occ_ref, orb, k * group, group)
        acc[k * rows : (k + 1) * rows, :] += jnp.dot(
            pairs, turned, preferred_element_type=jnp.float32
        )

    @pl.when(step == pl.num_programs(0) - 1)
    def _():
        out_ref[...] = acc[...].T


def project(occ, orbitals, potentials, start):
    slots, width = occ.shape
    stored = orbitals.shape[0]
    nv = potentials.shape[0]
    block = min(1024, width)
    shift = start // block
    pairs = slots * stored
    return pl.pallas_call(
        functools.partial(project_kernel, max(1, 256 // stored)),
        out_shape=jax.ShapeDtypeStruct((nv, pairs), jnp.float32),
        grid=(width // block,),
        in_specs=[
            pl.BlockSpec((slots, block), lambda s: (0, s)),
            pl.BlockSpec((stored, block), lambda s: (0, s + shift)),
            pl.BlockSpec((nv, block), lambda s: (0, s + shift)),
        ],
        out_specs=pl.BlockSpec((nv, pairs), lambda s: (0, 0)),
        scratch_shapes=[pltpu.VMEM((pairs, nv), jnp.float32)],
        compiler_params=pltpu.CompilerParams(vmem_limit_bytes=VMEM),
        cost_estimate=pl.CostEstimate(
            flops=2 * pairs * nv * width * 3,
            bytes_accessed=2 * width * (slots + stored + nv),
            transcendentals=0,
        ),
        name="project",
    )(occ, orbitals, potentials)


def respond_kernel(group, guess_ref, occ_ref, orb_ref, out_ref):
    orb = orb_ref[...]
    rows = group * orb.shape[0]
    total = None
    for k in range(occ_ref.shape[0] // group):
        pairs = pair_rows(occ_ref, orb, k * group, group)
        term = jnp.dot(
            guess_ref[:, k * rows : (k + 1) * rows], pairs, preferred_element_type=jnp.float32
        )
        total = term if total is None else total + term
    out_ref[...] = total


def respond(guess, occ, orbitals, start, occ_start, width):
    slots = occ.shape[0]
    stored = orbitals.shape[0]
    nv, pairs = guess.shape
    block = min(512, width)
    shift = start // block
    occ_shift = occ_start // block
    return pl.pallas_call(
        functools.partial(respond_kernel, max(1, 256 // stored)),
        out_shape=jax.ShapeDtypeStruct((nv, width), jnp.float32),
        grid=(width // block,),
        in_specs=[
            pl.BlockSpec((nv, pairs), lambda s: (0, 0)),
            pl.BlockSpec((slots, block), lambda s: (0, s + occ_shift)),
            pl.BlockSpec((stored, block), lambda s: (0, s + shift)),
        ],
        out_specs=pl.BlockSpec((nv, block), lambda s: (0, s)),
        compiler_params=pltpu.CompilerParams(vmem_limit_bytes=VMEM),
        cost_estimate=pl.CostEstimate(
            flops=2 * pairs * nv * width * 3,
            bytes_accessed=2 * width * (slots + stored) + 4 * nv * width,
            transcendentals=0,
        ),
        name="respond",
    )(guess, occ, orbitals)


def owner_order(nv, count, order):
    per = nv // count
    owners = []
    for place in range(count):
        owner = 0
        for depth, bit in enumerate(order):
            if (place >> (len(order) - 1 - depth)) & 1:
                owner |= bit
        owners.append(owner)
    return np.concatenate([np.arange(per) + o * per for o in owners])


def body(potentials, orbitals, levels, occ_index, coul_rows, coul_cols):
    nv, points_dev = potentials.shape
    volume = points_dev * lax.axis_size("cell")
    orb_count = lax.axis_size("orb")
    my_rank = lax.axis_index("orb")
    per_orb = orbitals.shape[0]
    slots = occ_index.shape[0]
    orb_bits = bits_of("orb")
    cell_bits = bits_of("cell")
    orders = [orb_bits, orb_bits[1:] + orb_bits[:1]]

    labels = jnp.arange(levels.shape[0], dtype=jnp.int32)
    marked = jnp.any(occ_index[:, None] == labels[None, :], axis=0)
    empty_all = 1.0 - marked.astype(jnp.float32)
    occ_hot = (occ_index[:, None] == labels[None, :]).astype(jnp.float32)
    occ_level = jnp.sum(occ_hot * levels[None, :], axis=1)
    basis_level = lax.dynamic_slice_in_dim(levels, my_rank * per_orb, per_orb)
    basis_empty = lax.dynamic_slice_in_dim(empty_all, my_rank * per_orb, per_orb)
    weights = -2.0 * basis_empty[None, :] / (occ_level[:, None] + basis_level[None, :])
    weights = (weights / volume).reshape(1, -1)

    owned_ids = my_rank * per_orb + jnp.arange(per_orb, dtype=jnp.int32)
    picker = (occ_index[:, None] == owned_ids[None, :]).astype(jnp.bfloat16)

    chunk = points_dev // GATHER_CHUNKS
    occ_parts = []
    for g in range(GATHER_CHUNKS):
        piece = jnp.dot(
            picker,
            orbitals[:, g * chunk : (g + 1) * chunk],
            preferred_element_type=jnp.float32,
        ).astype(jnp.bfloat16)
        order = orders[g % 2]
        for bit in order:
            piece = halve(piece, "orb", bit, 1)
        for bit in order[::-1]:
            piece = double(piece, "orb", bit, 1)
        occ_parts.append(piece)

    inter = None
    for g in range(GATHER_CHUNKS):
        part = project(occ_parts[g], orbitals, potentials, g * chunk)
        inter = part if inter is None else inter + part
    scale = weights
    for bit in cell_bits:
        inter = halve(inter, "cell", bit, 1)
        half = scale.shape[1] // 2
        scale = lax.dynamic_slice_in_dim(scale, upper("cell", bit) * half, half, 1)
    guess = (inter * scale).astype(jnp.bfloat16)
    for bit in cell_bits[::-1]:
        guess = double(guess, "cell", bit, 1)

    width = points_dev // RESPONSE_CHUNKS
    guesses = []
    for order in orders:
        rows = owner_order(nv, orb_count, order)
        place = jnp.asarray(rows[:, None] == np.arange(nv)[None, :], jnp.bfloat16)
        guesses.append(
            jnp.dot(place, guess, preferred_element_type=jnp.float32).astype(jnp.bfloat16)
        )
    owned = []
    for r in range(RESPONSE_CHUNKS):
        start = r * width
        part = respond(
            guesses[r % 2], occ_parts[start // chunk], orbitals, start, start % chunk, width
        )
        for bit in orders[r % 2]:
            part = halve(part, "orb", bit, 0, jnp.bfloat16)
        owned.append(part)
    owned_sum = jnp.concatenate(owned, 1)

    row_count = points_dev // SIDE
    plane_rows = owned_sum.reshape(owned_sum.shape[0], row_count, SIDE)
    by_columns = jnp.einsum("vrc,dc->vrd", plane_rows, coul_cols, precision=lax.Precision.HIGHEST)
    mixed_rows = jnp.einsum(
        "ab,vbc->vac",
        coul_rows,
        lax.all_to_all(by_columns, "cell", split_axis=2, concat_axis=1, tiled=True),
        precision=lax.Precision.HIGHEST,
    )
    return lax.all_to_all(mixed_rows, "cell", split_axis=1, concat_axis=2, tiled=True)


def solution(mesh):
    placed = (P(None, "cell"), P("orb", "cell"), P(), P(), P(), P())
    return jax.shard_map(
        body, mesh=mesh, in_specs=placed, out_specs=P("orb", "cell", None), check_vma=False
    )
```

time: 715 us -> 289 us (0.40)
  the two profiles are of different devices: /device:TPU:10 before, /device:TPU:0 now
where the time goes in v1:
time: 289 us; the launch traced here: 287 us
  waiting for transfers between devices  102 us (35%)
  Pallas kernels  79.5 us (28%)
  starting transfers between devices  38.4 us (13%)
  blocking collectives  28.4 us (10%)
  local copies, waits for them, and re-layouts  19.7 us (7%)
  other arithmetic  12.1 us (4%)
  matrix products  6.46 us (2%)
    ppermute x28, waiting for transfers between devices, swap(): return lax.ppermute(x, axis, [(s, s ^ bit) for s in range(n)])  102 us
    pallas_call x2, Pallas kernels, project(): pl.pallas_call(functools.partial(project_kernel, max(1, 256 // stored)),...  43.9 us
    ppermute x28, starting transfers between devices, swap(): return lax.ppermute(x, axis, [(s, s ^ bit) for s in range(n)])  38.4 us
    pallas_call x4, Pallas kernels, respond(): pl.pallas_call(functools.partial(respond_kernel, max(1, 256 // stored)),...  35.6 us
    all_to_all x1, blocking collectives, body(): lax.all_to_all(by_columns, 'cell', split_axis=2, concat_axis=1, tiled=True)  14.4 us
    all_to_all x1, blocking collectives, body(): lax.all_to_all(mixed_rows, 'cell', split_axis=1, concat_axis=2, tiled=True)  14 us
  transfers between devices with their start and end apart: 28, of which 20 were waited for; matrix products, arithmetic and copies ran while one was open for 2% of the time, Pallas kernels for 8%

profile of v1, /device:TPU:0, one launch (start us, length us, event | category | flops | bytes accessed | tf_op | source)
XLA Modules:
  0.0 286.9 jit_solution(8551197746883510916)
XLA Ops:
  0.0 1.9 convolution_convert_fusion
  2.7 3.1 %collective-permute-start.6 = (bf16[64,4096]{1,0:T(8,128)(2,1)}, bf16[64,4096]{1,0:T(8,128)(2,1)S(1)}, u32[]{:S(2)}, u32[]{:S(2)}) collective-permute-start(bf16[64,4096]{1,0:T(8,128)(2,1)} %constant_dynamic-slice_fusion.5), channel_id=1, source_target_pairs={{0,8},{4,12},{8,0},{12,4},{16,24},{20,28},{24,16},{28,20},{1,9},{5... | collective-permute-start | bytes 1572872 | tf_op jit(solution)/shard_map/ppermute | solution.py:19
  7.1 1.5 collective-permute-start
  8.6 9.3 %collective-permute-done.6 = bf16[64,4096]{1,0:T(8,128)(2,1)S(1)} collective-permute-done((bf16[64,4096]{1,0:T(8,128)(2,1)}, bf16[64,4096]{1,0:T(8,128)(2,1)S(1)}, u32[]{:S(2)}, u32[]{:S(2)}) %collective-permute-start.6) | collective-permute-done | bytes 524320 | tf_op jit(solution)/shard_map/ppermute | solution.py:19
  18.1 2.8 collective-permute-start.7
  21.1 1.6 collective-permute-start.1
  22.7 9.5 %collective-permute-done.7 = bf16[64,2048]{1,0:T(8,128)(2,1)S(1)} collective-permute-done((bf16[64,2048]{1,0:T(8,128)(2,1)S(1)}, bf16[64,2048]{1,0:T(8,128)(2,1)S(1)}, u32[]{:S(2)}, u32[]{:S(2)}) %collective-permute-start.7) | collective-permute-done | bytes 262176 | tf_op jit(solution)/shard_map/ppermute | solution.py:19
  34.2 3.2 %collective-permute-done.8 = bf16[64,1024]{1,0:T(8,128)(2,1)S(1)} collective-permute-done((bf16[64,1024]{1,0:T(8,128)(2,1)S(1)}, bf16[64,1024]{1,0:T(8,128)(2,1)S(1)}, u32[]{:S(2)}, u32[]{:S(2)}) %collective-permute-start.8) | collective-permute-done | bytes 131104 | tf_op jit(solution)/shard_map/ppermute | solution.py:19
  38.9 4.6 %collective-permute-done.2 = bf16[64,1024]{1,0:T(8,128)(2,1)S(1)} collective-permute-done((bf16[64,1024]{1,0:T(8,128)(2,1)S(1)}, bf16[64,1024]{1,0:T(8,128)(2,1)S(1)}, u32[]{:S(2)}, u32[]{:S(2)}) %collective-permute-start.2) | collective-permute-done | bytes 131104 | tf_op jit(solution)/shard_map/ppermute | solution.py:19
  43.6 3.0 %collective-permute-start.10 = (bf16[64,2048]{1,0:T(8,128)(2,1)S(1)}, bf16[64,2048]{1,0:T(8,128)(2,1)S(1)}, u32[]{:S(2)}, u32[]{:S(2)}) collective-permute-start(bf16[64,2048]{1,0:T(8,128)(2,1)S(1)} %pad_maximum_fusion.10), channel_id=1, source_target_pairs={{0,16},{4,20},{8,24},{12,28},{16,0},{20,4},{24,8},{28,12},{1,17},{... | collective-permute-start | bytes 786440 | tf_op jit(solution)/shard_map/ppermute | solution.py:19
  46.6 7.6 %collective-permute-done.3 = bf16[64,1024]{1,0:T(8,128)(2,1)S(1)} collective-permute-done((bf16[64,1024]{1,0:T(8,128)(2,1)S(1)}, bf16[64,1024]{1,0:T(8,128)(2,1)S(1)}, u32[]{:S(2)}, u32[]{:S(2)}) %collective-permute-start.3) | collective-permute-done | bytes 131104 | tf_op jit(solution)/shard_map/ppermute | solution.py:19
  54.8 4.3 %collective-permute-done.10 = bf16[64,2048]{1,0:T(8,128)(2,1)S(1)} collective-permute-done((bf16[64,2048]{1,0:T(8,128)(2,1)S(1)}, bf16[64,2048]{1,0:T(8,128)(2,1)S(1)}, u32[]{:S(2)}, u32[]{:S(2)}) %collective-permute-start.10) | collective-permute-done | bytes 262176 | tf_op jit(solution)/shard_map/ppermute | solution.py:19
  59.4 5.4 %collective-permute-done.4 = bf16[64,2048]{1,0:T(8,128)(2,1)S(1)} collective-permute-done((bf16[64,2048]{1,0:T(8,128)(2,1)S(1)}, bf16[64,2048]{1,0:T(8,128)(2,1)S(1)}, u32[]{:S(2)}, u32[]{:S(2)}) %collective-permute-start.4) | collective-permute-done | bytes 262176 | tf_op jit(solution)/shard_map/ppermute | solution.py:19
  65.0 7.1 %collective-permute-done.11 = bf16[64,4096]{1,0:T(8,128)(2,1)S(1)} collective-permute-done((bf16[64,4096]{1,0:T(8,128)(2,1)S(1)}, bf16[64,4096]{1,0:T(8,128)(2,1)S(1)}, u32[]{:S(2)}, u32[]{:S(2)}) %collective-permute-start.11) | collective-permute-done | bytes 524320 | tf_op jit(solution)/shard_map/ppermute | solution.py:19
  73.4 21.9 %project.3 = f32[96,4096]{1,0:T(8,128)} custom-call(bf16[64,8192]{1,0:T(8,128)(2,1)} %pad_maximum_fusion.1.occ_ref, bf16[64,16384]{1,0:T(8,128)(2,1)} %orb_ref.11, bf16[96,16384]{1,0:T(8,128)(2,1)} %pot_ref.3), custom_call_target="tpu_custom_call" | custom-call | flops 19327352832 | bytes 3670016 | tf_op jit(solution)/shard_map/project/pallas_call | solution.py:79
  96.5 22.0 %project.2 = f32[96,4096]{1,0:T(8,128)} custom-call(bf16[64,8192]{1,0:T(8,128)(2,1)} %pad_maximum_fusion.occ_ref, bf16[64,16384]{1,0:T(8,128)(2,1)} %orb_ref.11, bf16[96,16384]{1,0:T(8,128)(2,1)} %pot_ref.3), custom_call_target="tpu_custom_call" | custom-call | flops 19327352832 | bytes 3670016 | tf_op jit(solution)/shard_map/project/pallas_call | solution.py:79
  118.5 1.6 add.269
  121.0 1.6 collective-permute-done.12
  122.7 1.7 collective-permute-start.13
  124.8 9.1 %collective-permute-done.13 = f32[96,1024]{1,0:T(8,128)S(1)} collective-permute-done((f32[96,1024]{1,0:T(8,128)S(1)}, f32[96,1024]{1,0:T(8,128)S(1)}, u32[]{:S(2)}, u32[]{:S(2)}) %collective-permute-start.13) | collective-permute-done | bytes 393248 | tf_op jit(solution)/shard_map/ppermute | solution.py:19
  133.9 1.7 collective-permute-start.14
  135.6 4.4 %collective-permute-done.14 = bf16[96,1024]{1,0:T(8,128)(2,1)S(1)} collective-permute-done((bf16[96,1024]{1,0:T(8,128)(2,1)S(1)}, bf16[96,1024]{1,0:T(8,128)(2,1)S(1)}, u32[]{:S(2)}, u32[]{:S(2)}) %collective-permute-start.14) | collective-permute-done | bytes 196640 | tf_op jit(solution)/shard_map/ppermute | solution.py:19
  140.3 1.6 collective-permute-done.15
  143.4 8.8 %respond.4 = f32[96,4096]{1,0:T(8,128)} custom-call(bf16[96,4096]{1,0:T(8,128)(2,1)} %fusion.guess_ref, bf16[64,8192]{1,0:T(8,128)(2,1)} %pad_maximum_fusion.occ_ref, bf16[64,16384]{1,0:T(8,128)(2,1)} %orb_ref.11), custom_call_target="tpu_custom_call" | custom-call | flops 9663676416 | bytes 2621440 | tf_op jit(solution)/shard_map/respond/pallas_call | solution.py:120
  152.2 8.9 %respond.6 = f32[96,4096]{1,0:T(8,128)} custom-call(bf16[96,4096]{1,0:T(8,128)(2,1)} %fusion.guess_ref, bf16[64,8192]{1,0:T(8,128)(2,1)} %pad_maximum_fusion.1.occ_ref, bf16[64,16384]{1,0:T(8,128)(2,1)} %orb_ref.11), custom_call_target="tpu_custom_call" | custom-call | flops 9663676416 | bytes 2621440 | tf_op jit(solution)/shard_map/respond/pallas_call | solution.py:120
  162.3 8.9 %respond.5 = f32[96,4096]{1,0:T(8,128)} custom-call(bf16[96,4096]{1,0:T(8,128)(2,1)} %fusion.1.guess_ref, bf16[64,8192]{1,0:T(8,128)(2,1)} %pad_maximum_fusion.occ_ref, bf16[64,16384]{1,0:T(8,128)(2,1)} %orb_ref.11), custom_call_target="tpu_custom_call" | custom-call | flops 9663676416 | bytes 2621440 | tf_op jit(solution)/shard_map/respond/pallas_call | solution.py:120
  171.2 9.0 %respond.7 = f32[96,4096]{1,0:T(8,128)} custom-call(bf16[96,4096]{1,0:T(8,128)(2,1)} %fusion.1.guess_ref, bf16[64,8192]{1,0:T(8,128)(2,1)} %pad_maximum_fusion.1.occ_ref, bf16[64,16384]{1,0:T(8,128)(2,1)} %orb_ref.11), custom_call_target="tpu_custom_call" | custom-call | flops 9663676416 | bytes 2621440 | tf_op jit(solution)/shard_map/respond/pallas_call | solution.py:120
  180.3 3.4 %collective-permute-start.16 = (bf16[48,4096]{1,0:T(8,128)(2,1)S(1)}, bf16[48,4096]{1,0:T(8,128)(2,1)S(1)}, u32[]{:S(2)}, u32[]{:S(2)}) collective-permute-start(bf16[48,4096]{1,0:T(8,128)(2,1)S(1)} %dynamic-slice_convert_fusion.3), channel_id=1, source_target_pairs={{0,4},{4,0},{8,12},{12,8},{16,20},{20,16},{24,28},{28,24},{1,5},{5... | collective-permute-start | bytes 1179656 | tf_op jit(solution)/shard_map/ppermute | solution.py:19
  184.0 2.1 collective-permute-start.25
  186.1 7.6 %collective-permute-done.16 = bf16[48,4096]{1,0:T(8,128)(2,1)S(1)} collective-permute-done((bf16[48,4096]{1,0:T(8,128)(2,1)S(1)}, bf16[48,4096]{1,0:T(8,128)(2,1)S(1)}, u32[]{:S(2)}, u32[]{:S(2)}) %collective-permute-start.16) | collective-permute-done | bytes 393248 | tf_op jit(solution)/shard_map/ppermute | solution.py:19
  193.8 1.9 collective-permute-done.19
  195.9 3.6 %collective-permute-start.20 = (bf16[24,4096]{1,0:T(8,128)(2,1)S(1)}, bf16[24,4096]{1,0:T(8,128)(2,1)S(1)}, u32[]{:S(2)}, u32[]{:S(2)}) collective-permute-start(bf16[24,4096]{1,0:T(8,128)(2,1)S(1)} %dynamic-slice_convert_fusion.6), channel_id=1, source_target_pairs={{0,16},{4,20},{8,24},{12,28},{16,0},{20,4},{24,8},{28,12},{1,17},{... | collective-permute-start | bytes 589832 | tf_op jit(solution)/shard_map/ppermute | solution.py:19
  199.5 2.0 collective-permute-done.22
  201.7 6.7 %collective-permute-done.25 = bf16[48,4096]{1,0:T(8,128)(2,1)S(1)} collective-permute-done((bf16[48,4096]{1,0:T(8,128)(2,1)S(1)}, bf16[48,4096]{1,0:T(8,128)(2,1)S(1)}, u32[]{:S(2)}, u32[]{:S(2)}) %collective-permute-start.25) | collective-permute-done | bytes 393248 | tf_op jit(solution)/shard_map/ppermute | solution.py:19
  208.5 3.1 %collective-permute-start.26 = (bf16[24,4096]{1,0:T(8,128)(2,1)S(1)}, bf16[24,4096]{1,0:T(8,128)(2,1)S(1)}, u32[]{:S(2)}, u32[]{:S(2)}) collective-permute-start(bf16[24,4096]{1,0:T(8,128)(2,1)S(1)} %dynamic-slice_convert_fusion.4), channel_id=1, source_target_pairs={{0,16},{4,20},{8,24},{12,28},{16,0},{20,4},{24,8},{28,12},{1,17},{... | collective-permute-start | bytes 589832 | tf_op jit(solution)/shard_map/ppermute | solution.py:19
  211.6 1.6 collective-permute-done.17
  213.3 5.0 %collective-permute-start.18 = (bf16[12,4096]{1,0:T(8,128)(2,1)S(1)}, bf16[12,4096]{1,0:T(8,128)(2,1)S(1)}, u32[]{:S(2)}, u32[]{:S(2)}) collective-permute-start(bf16[12,4096]{1,0:T(8,128)(2,1)S(1)} %dynamic-slice_convert_fusion.11), channel_id=1, source_target_pairs={{0,16},{4,20},{8,24},{12,28},{16,0},{20,4},{24,8},{28,12},{1,17},{... | collective-permute-start | bytes 294920 | tf_op jit(solution)/shard_map/ppermute | solution.py:19
  218.5 2.0 collective-permute-done.23
  221.9 9.8 %collective-permute-done.18 = bf16[12,4096]{1,0:T(8,128)(2,1)S(1)} collective-permute-done((bf16[12,4096]{1,0:T(8,128)(2,1)S(1)}, bf16[12,4096]{1,0:T(8,128)(2,1)S(1)}, u32[]{:S(2)}, u32[]{:S(2)}) %collective-permute-start.18) | collective-permute-done | bytes 98336 | tf_op jit(solution)/shard_map/ppermute | solution.py:19
  231.8 2.2 collective-permute-done.24
  237.7 14.4 %all_to_all.36 = f32[4,1,49152]{2,1,0:T(1,128)S(1)} all-to-all(f32[4,1,49152]{2,1,0:T(1,128)S(1)} %reshape.57), channel_id=1, replica_groups=mesh['orb'=8,'cell'=4] {'cell'}, dimensions={0} | all-to-all | bytes 1572864 | tf_op jit(solution)/shard_map/all_to_all | solution.py:229
  252.6 2.9 %reduce = f32[4,49152]{1,0:T(4,128)S(1)} reduce(f32[4,1,49152]{2,1,0:T(1,128)S(1)} %all_to_all.36, f32[]{:T(128)} %broadcast.41), dimensions={1}, to_apply=%all_to_all.26.reduce_sub_computation | reduce | bytes 1572868 | tf_op jit(solution)/shard_map/all_to_all | solution.py:229
  256.4 2.2 copy.21
  258.6 2.3 all_to_all.29
  264.0 14.0 %all_to_all.37 = f32[4,1,49152]{2,1,0:T(1,128)S(1)} all-to-all(f32[4,1,49152]{2,1,0:T(1,128)S(1)} %reshape.59), channel_id=1, replica_groups=mesh['orb'=8,'cell'=4] {'cell'}, dimensions={0} | all-to-all | bytes 1572864 | tf_op jit(solution)/shard_map/all_to_all | solution.py:232
  278.1 2.9 %reduce.1 = f32[4,49152]{1,0:T(4,128)S(1)} reduce(f32[4,1,49152]{2,1,0:T(1,128)S(1)} %all_to_all.37, f32[]{:T(128)} %broadcast.41), dimensions={1}, to_apply=%all_to_all.30.reduce_sub_computation | reduce | bytes 1572868 | tf_op jit(solution)/shard_map/all_to_all | solution.py:232
  281.8 2.2 copy.18
  284.0 3.0 %all_to_all.33 = f32[12,64,256]{2,1,0:T(8,128)} reshape(f32[12,64,4,64]{3,2,1,0:T(4,128)} %copy.18) | data formatting | bytes 1572864 | tf_op jit(solution)/shard_map/all_to_all | solution.py:232
  (126 shorter events, 25.2 us)
Async XLA Ops:
  0.0 234.5 %copy-start = (f32[256,256]{1,0:T(8,128)S(1)}, f32[256,256]{1,0:T(8,128)}, u32[]{:S(2)}) copy-start(f32[256,256]{1,0:T(8,128)} %param.13) | copy-start | bytes 786436
  0.0 5.8 %copy-start.1 = (bf16[64,16384]{1,0:T(8,128)(2,1)S(1)}, bf16[64,16384]{1,0:T(8,128)(2,1)}, u32[]{:S(2)}) copy-start(bf16[64,16384]{1,0:T(8,128)(2,1)} %orb_ref.11) | copy-start | bytes 6291460
  0.0 5.8 %copy-start.10 = (s32[64]{0:T(128)S(1)}, s32[64]{0:T(128)}, u32[]{:S(2)}) copy-start(s32[64]{0:T(128)} %param.11) | copy-start | bytes 772
  2.7 15.2 %collective-permute-start.6 = (bf16[64,4096]{1,0:T(8,128)(2,1)}, bf16[64,4096]{1,0:T(8,128)(2,1)S(1)}, u32[]{:S(2)}, u32[]{:S(2)}) collective-permute-start(bf16[64,4096]{1,0:T(8,128)(2,1)} %constant_dynamic-slice_fusion.5), channel_id=1, source_target_pairs={{0,8},{4,12},{8,0},{12,4},{16,24},{20,28},{24,16},{28,20},{1,9},{5... | collective-permute-start | bytes 1572872 | tf_op jit(solution)/shard_map/ppermute | solution.py:19
  7.1 13.8 %collective-permute-start = (bf16[64,4096]{1,0:T(8,128)(2,1)}, bf16[64,4096]{1,0:T(8,128)(2,1)S(1)}, u32[]{:S(2)}, u32[]{:S(2)}) collective-permute-start(bf16[64,4096]{1,0:T(8,128)(2,1)} %constant_dynamic-slice_fusion.8), channel_id=1, source_target_pairs={{0,4},{4,0},{8,12},{12,8},{16,20},{20,16},{24,28},{28,24},{1,5},{5... | collective-permute-start | bytes 1572872 | tf_op jit(solution)/shard_map/ppermute | solution.py:19
  18.1 14.2 %collective-permute-start.7 = (bf16[64,2048]{1,0:T(8,128)(2,1)S(1)}, bf16[64,2048]{1,0:T(8,128)(2,1)S(1)}, u32[]{:S(2)}, u32[]{:S(2)}) collective-permute-start(bf16[64,2048]{1,0:T(8,128)(2,1)S(1)} %constant_dynamic-slice_fusion.4), channel_id=1, source_target_pairs={{0,16},{4,20},{8,24},{12,28},{16,0},{20,4},{24,8},{28,12},{1,17},{... | collective-permute-start | bytes 786440 | tf_op jit(solution)/shard_map/ppermute | solution.py:19
  21.1 12.7 %collective-permute-start.1 = (bf16[64,2048]{1,0:T(8,128)(2,1)S(1)}, bf16[64,2048]{1,0:T(8,128)(2,1)S(1)}, u32[]{:S(2)}, u32[]{:S(2)}) collective-permute-start(bf16[64,2048]{1,0:T(8,128)(2,1)S(1)} %constant_dynamic-slice_fusion.7), channel_id=1, source_target_pairs={{0,8},{4,12},{8,0},{12,4},{16,24},{20,28},{24,16},{28,20},{1,9},{5... | collective-permute-start | bytes 786440 | tf_op jit(solution)/shard_map/ppermute | solution.py:19
  32.4 5.0 %collective-permute-start.8 = (bf16[64,1024]{1,0:T(8,128)(2,1)S(1)}, bf16[64,1024]{1,0:T(8,128)(2,1)S(1)}, u32[]{:S(2)}, u32[]{:S(2)}) collective-permute-start(bf16[64,1024]{1,0:T(8,128)(2,1)S(1)} %constant_dynamic-slice_fusion.3), channel_id=1, source_target_pairs={{0,4},{4,0},{8,12},{12,8},{16,20},{20,16},{24,28},{28,24},{1,5},{5... | collective-permute-start | bytes 393224 | tf_op jit(solution)/shard_map/ppermute | solution.py:19
  33.9 9.6 %collective-permute-start.2 = (bf16[64,1024]{1,0:T(8,128)(2,1)S(1)}, bf16[64,1024]{1,0:T(8,128)(2,1)S(1)}, u32[]{:S(2)}, u32[]{:S(2)}) collective-permute-start(bf16[64,1024]{1,0:T(8,128)(2,1)S(1)} %constant_dynamic-slice_fusion.6), channel_id=1, source_target_pairs={{0,16},{4,20},{8,24},{12,28},{16,0},{20,4},{24,8},{28,12},{1,17},{... | collective-permute-start | bytes 393224 | tf_op jit(solution)/shard_map/ppermute | solution.py:19
  37.4 6.1 %collective-permute-start.9 = (bf16[64,1024]{1,0:T(8,128)(2,1)S(1)}, bf16[64,1024]{1,0:T(8,128)(2,1)S(1)}, u32[]{:S(2)}, u32[]{:S(2)}) collective-permute-start(bf16[64,1024]{1,0:T(8,128)(2,1)S(1)} %dynamic-slice_add_fusion.5), channel_id=1, source_target_pairs={{0,4},{4,0},{8,12},{12,8},{16,20},{20,16},{24,28},{28,24},{1,5},{5... | collective-permute-start | bytes 393224 | tf_op jit(solution)/shard_map/ppermute | solution.py:19
  43.5 10.7 %collective-permute-start.3 = (bf16[64,1024]{1,0:T(8,128)(2,1)S(1)}, bf16[64,1024]{1,0:T(8,128)(2,1)S(1)}, u32[]{:S(2)}, u32[]{:S(2)}) collective-permute-start(bf16[64,1024]{1,0:T(8,128)(2,1)S(1)} %dynamic-slice_add_fusion.6), channel_id=1, source_target_pairs={{0,16},{4,20},{8,24},{12,28},{16,0},{20,4},{24,8},{28,12},{1,17},{... | collective-permute-start | bytes 393224 | tf_op jit(solution)/shard_map/ppermute | solution.py:19
  43.6 15.5 %collective-permute-start.10 = (bf16[64,2048]{1,0:T(8,128)(2,1)S(1)}, bf16[64,2048]{1,0:T(8,128)(2,1)S(1)}, u32[]{:S(2)}, u32[]{:S(2)}) collective-permute-start(bf16[64,2048]{1,0:T(8,128)(2,1)S(1)} %pad_maximum_fusion.10), channel_id=1, source_target_pairs={{0,16},{4,20},{8,24},{12,28},{16,0},{20,4},{24,8},{28,12},{1,17},{... | collective-permute-start | bytes 786440 | tf_op jit(solution)/shard_map/ppermute | solution.py:19
  54.2 10.5 %collective-permute-start.4 = (bf16[64,2048]{1,0:T(8,128)(2,1)S(1)}, bf16[64,2048]{1,0:T(8,128)(2,1)S(1)}, u32[]{:S(2)}, u32[]{:S(2)}) collective-permute-start(bf16[64,2048]{1,0:T(8,128)(2,1)S(1)} %pad_maximum_fusion.9), channel_id=1, source_target_pairs={{0,8},{4,12},{8,0},{12,4},{16,24},{20,28},{24,16},{28,20},{1,9},{5... | collective-permute-start | bytes 786440 | tf_op jit(solution)/shard_map/ppermute | solution.py:19
  59.3 12.8 %collective-permute-start.11 = (bf16[64,4096]{1,0:T(8,128)(2,1)S(1)}, bf16[64,4096]{1,0:T(8,128)(2,1)S(1)}, u32[]{:S(2)}, u32[]{:S(2)}) collective-permute-start(bf16[64,4096]{1,0:T(8,128)(2,1)S(1)} %pad_maximum_fusion.5), channel_id=1, source_target_pairs={{0,8},{4,12},{8,0},{12,4},{16,24},{20,28},{24,16},{28,20},{1,9},{5... | collective-permute-start | bytes 1572872 | tf_op jit(solution)/shard_map/ppermute | solution.py:19
  64.9 30.4 %collective-permute-start.5 = (bf16[64,4096]{1,0:T(8,128)(2,1)S(1)}, bf16[64,4096]{1,0:T(8,128)(2,1)S(1)}, u32[]{:S(2)}, u32[]{:S(2)}) collective-permute-start(bf16[64,4096]{1,0:T(8,128)(2,1)S(1)} %pad_maximum_fusion.4), channel_id=1, source_target_pairs={{0,4},{4,0},{8,12},{12,8},{16,20},{20,16},{24,28},{28,24},{1,5},{5... | collective-permute-start | bytes 1572872 | tf_op jit(solution)/shard_map/ppermute | solution.py:19
  96.5 22.0 %copy-start.2 = (f32[96,4096]{1,0:T(8,128)S(1)}, f32[96,4096]{1,0:T(8,128)}, u32[]{:S(2)}) copy-start(f32[96,4096]{1,0:T(8,128)} %project.3) | copy-start | bytes 4718596
  120.1 0.7 copy-start.11
  120.2 2.4 collective-permute-start.12
  122.7 11.2 %collective-permute-start.13 = (f32[96,1024]{1,0:T(8,128)S(1)}, f32[96,1024]{1,0:T(8,128)S(1)}, u32[]{:S(2)}, u32[]{:S(2)}) collective-permute-start(f32[96,1024]{1,0:T(8,128)S(1)} %constant_dynamic-slice_fusion.1), channel_id=1, source_target_pairs={{0,2},{1,3},{2,0},{3,1},{4,6},{5,7},{6,4},{7,5},{8,10},{9,11},{10,... | collective-permute-start | bytes 1179656 | tf_op jit(solution)/shard_map/ppermute | solution.py:19
  133.9 6.2 %collective-permute-start.14 = (bf16[96,1024]{1,0:T(8,128)(2,1)S(1)}, bf16[96,1024]{1,0:T(8,128)(2,1)S(1)}, u32[]{:S(2)}, u32[]{:S(2)}) collective-permute-start(bf16[96,1024]{1,0:T(8,128)(2,1)S(1)} %multiply_convert_fusion), channel_id=1, source_target_pairs={{0,2},{1,3},{2,0},{3,1},{4,6},{5,7},{6,4},{7,5},{8,10},{9,11},{10,... | collective-permute-start | bytes 589832 | tf_op jit(solution)/shard_map/ppermute | solution.py:19
  135.6 6.5 %copy-start.9 = (bf16[96,96]{1,0:T(8,128)(2,1)S(1)}, bf16[96,96]{1,0:T(8,128)(2,1)}, u32[]{:S(2)}) copy-start(bf16[96,96]{1,0:T(8,128)(2,1)} %constant.228.clone) | copy-start | bytes 55300
  140.2 1.8 collective-permute-start.15
  152.2 8.9 %copy-start.8 = (bf16[96,96]{1,0:T(8,128)(2,1)S(1)}, bf16[96,96]{1,0:T(8,128)(2,1)}, u32[]{:S(2)}) copy-start(bf16[96,96]{1,0:T(8,128)(2,1)} %constant.229.clone) | copy-start | bytes 55300
  171.2 9.0 %copy-start.6 = (f32[96,4096]{1,0:T(8,128)S(1)}, f32[96,4096]{1,0:T(8,128)}, u32[]{:S(2)}) copy-start(f32[96,4096]{1,0:T(8,128)} %respond.4) | copy-start | bytes 4718596
  171.2 12.5 %copy-start.5 = (f32[96,4096]{1,0:T(8,128)S(1)}, f32[96,4096]{1,0:T(8,128)}, u32[]{:S(2)}) copy-start(f32[96,4096]{1,0:T(8,128)} %respond.5) | copy-start | bytes 4718596
  171.2 12.6 %copy-start.4 = (f32[96,4096]{1,0:T(8,128)S(1)}, f32[96,4096]{1,0:T(8,128)}, u32[]{:S(2)}) copy-start(f32[96,4096]{1,0:T(8,128)} %respond.6) | copy-start | bytes 4718596
  180.2 3.8 %copy-start.3 = (f32[96,4096]{1,0:T(8,128)S(1)}, f32[96,4096]{1,0:T(8,128)}, u32[]{:S(2)}) copy-start(f32[96,4096]{1,0:T(8,128)} %respond.7) | copy-start | bytes 4718596
  180.3 13.4 %collective-permute-start.16 = (bf16[48,4096]{1,0:T(8,128)(2,1)S(1)}, bf16[48,4096]{1,0:T(8,128)(2,1)S(1)}, u32[]{:S(2)}, u32[]{:S(2)}) collective-permute-start(bf16[48,4096]{1,0:T(8,128)(2,1)S(1)} %dynamic-slice_convert_fusion.3), channel_id=1, source_target_pairs={{0,4},{4,0},{8,12},{12,8},{16,20},{20,16},{24,28},{28,24},{1,5},{5... | collective-permute-start | bytes 1179656 | tf_op jit(solution)/shard_map/ppermute | solution.py:19
  183.7 12.1 %collective-permute-start.19 = (bf16[48,4096]{1,0:T(8,128)(2,1)S(1)}, bf16[48,4096]{1,0:T(8,128)(2,1)S(1)}, u32[]{:S(2)}, u32[]{:S(2)}) collective-permute-start(bf16[48,4096]{1,0:T(8,128)(2,1)S(1)} %dynamic-slice_convert_fusion.2), channel_id=1, source_target_pairs={{0,8},{4,12},{8,0},{12,4},{16,24},{20,28},{24,16},{28,20},{1,9},{5... | collective-permute-start | bytes 1179656 | tf_op jit(solution)/shard_map/ppermute | solution.py:19
  183.9 17.7 %collective-permute-start.22 = (bf16[48,4096]{1,0:T(8,128)(2,1)S(1)}, bf16[48,4096]{1,0:T(8,128)(2,1)S(1)}, u32[]{:S(2)}, u32[]{:S(2)}) collective-permute-start(bf16[48,4096]{1,0:T(8,128)(2,1)S(1)} %dynamic-slice_convert_fusion.1), channel_id=1, source_target_pairs={{0,4},{4,0},{8,12},{12,8},{16,20},{20,16},{24,28},{28,24},{1,5},{5... | collective-permute-start | bytes 1179656 | tf_op jit(solution)/shard_map/ppermute | solution.py:19
  184.0 24.4 %collective-permute-start.25 = (bf16[48,4096]{1,0:T(8,128)(2,1)S(1)}, bf16[48,4096]{1,0:T(8,128)(2,1)S(1)}, u32[]{:S(2)}, u32[]{:S(2)}) collective-permute-start(bf16[48,4096]{1,0:T(8,128)(2,1)S(1)} %dynamic-slice_convert_fusion), channel_id=1, source_target_pairs={{0,8},{4,12},{8,0},{12,4},{16,24},{20,28},{24,16},{28,20},{1,9},{5... | collective-permute-start | bytes 1179656 | tf_op jit(solution)/shard_map/ppermute | solution.py:19
  193.7 19.5 %collective-permute-start.17 = (bf16[24,4096]{1,0:T(8,128)(2,1)S(1)}, bf16[24,4096]{1,0:T(8,128)(2,1)S(1)}, u32[]{:S(2)}, u32[]{:S(2)}) collective-permute-start(bf16[24,4096]{1,0:T(8,128)(2,1)S(1)} %dynamic-slice_convert_fusion.7), channel_id=1, source_target_pairs={{0,8},{4,12},{8,0},{12,4},{16,24},{20,28},{24,16},{28,20},{1,9},{5... | collective-permute-start | bytes 589832 | tf_op jit(solution)/shard_map/ppermute | solution.py:19
  195.9 22.5 %collective-permute-start.20 = (bf16[24,4096]{1,0:T(8,128)(2,1)S(1)}, bf16[24,4096]{1,0:T(8,128)(2,1)S(1)}, u32[]{:S(2)}, u32[]{:S(2)}) collective-permute-start(bf16[24,4096]{1,0:T(8,128)(2,1)S(1)} %dynamic-slice_convert_fusion.6), channel_id=1, source_target_pairs={{0,16},{4,20},{8,24},{12,28},{16,0},{20,4},{24,8},{28,12},{1,17},{... | collective-permute-start | bytes 589832 | tf_op jit(solution)/shard_map/ppermute | solution.py:19
  201.6 18.9 %collective-permute-start.23 = (bf16[24,4096]{1,0:T(8,128)(2,1)S(1)}, bf16[24,4096]{1,0:T(8,128)(2,1)S(1)}, u32[]{:S(2)}, u32[]{:S(2)}) collective-permute-start(bf16[24,4096]{1,0:T(8,128)(2,1)S(1)} %dynamic-slice_convert_fusion.5), channel_id=1, source_target_pairs={{0,8},{4,12},{8,0},{12,4},{16,24},{20,28},{24,16},{28,20},{1,9},{5... | collective-permute-start | bytes 589832 | tf_op jit(solution)/shard_map/ppermute | solution.py:19
  208.5 12.9 %collective-permute-start.26 = (bf16[24,4096]{1,0:T(8,128)(2,1)S(1)}, bf16[24,4096]{1,0:T(8,128)(2,1)S(1)}, u32[]{:S(2)}, u32[]{:S(2)}) collective-permute-start(bf16[24,4096]{1,0:T(8,128)(2,1)S(1)} %dynamic-slice_convert_fusion.4), channel_id=1, source_target_pairs={{0,16},{4,20},{8,24},{12,28},{16,0},{20,4},{24,8},{28,12},{1,17},{... | collective-permute-start | bytes 589832 | tf_op jit(solution)/shard_map/ppermute | solution.py:19
  213.3 18.4 %collective-permute-start.18 = (bf16[12,4096]{1,0:T(8,128)(2,1)S(1)}, bf16[12,4096]{1,0:T(8,128)(2,1)S(1)}, u32[]{:S(2)}, u32[]{:S(2)}) collective-permute-start(bf16[12,4096]{1,0:T(8,128)(2,1)S(1)} %dynamic-slice_convert_fusion.11), channel_id=1, source_target_pairs={{0,16},{4,20},{8,24},{12,28},{16,0},{20,4},{24,8},{28,12},{1,17},{... | collective-permute-start | bytes 294920 | tf_op jit(solution)/shard_map/ppermute | solution.py:19
  218.4 15.6 %collective-permute-start.21 = (bf16[12,4096]{1,0:T(8,128)(2,1)S(1)}, bf16[12,4096]{1,0:T(8,128)(2,1)S(1)}, u32[]{:S(2)}, u32[]{:S(2)}) collective-permute-start(bf16[12,4096]{1,0:T(8,128)(2,1)S(1)} %dynamic-slice_convert_fusion.10), channel_id=1, source_target_pairs={{0,4},{4,0},{8,12},{12,8},{16,20},{20,16},{24,28},{28,24},{1,5},{5... | collective-permute-start | bytes 294920 | tf_op jit(solution)/shard_map/ppermute | solution.py:19
  220.6 13.3 %collective-permute-start.24 = (bf16[12,4096]{1,0:T(8,128)(2,1)S(1)}, bf16[12,4096]{1,0:T(8,128)(2,1)S(1)}, u32[]{:S(2)}, u32[]{:S(2)}) collective-permute-start(bf16[12,4096]{1,0:T(8,128)(2,1)S(1)} %dynamic-slice_convert_fusion.9), channel_id=1, source_target_pairs={{0,16},{4,20},{8,24},{12,28},{16,0},{20,4},{24,8},{28,12},{1,17},{... | collective-permute-start | bytes 294920 | tf_op jit(solution)/shard_map/ppermute | solution.py:19
  221.5 12.5 %collective-permute-start.27 = (bf16[12,4096]{1,0:T(8,128)(2,1)S(1)}, bf16[12,4096]{1,0:T(8,128)(2,1)S(1)}, u32[]{:S(2)}, u32[]{:S(2)}) collective-permute-start(bf16[12,4096]{1,0:T(8,128)(2,1)S(1)} %dynamic-slice_convert_fusion.8), channel_id=1, source_target_pairs={{0,4},{4,0},{8,12},{12,8},{16,20},{20,16},{24,28},{28,24},{1,5},{5... | collective-permute-start | bytes 294920 | tf_op jit(solution)/shard_map/ppermute | solution.py:19
  258.5 2.3 copy-start.7

commit v2 on v1

--- a/solution.py
+++ b/solution.py
@@ -137,6 +137,31 @@
     )(guess, occ, orbitals)
 
 
+def mix_kernel(mixer_ref, stack_ref, out_ref):
+    out_ref[0] = jnp.dot(
+        mixer_ref[...],
+        stack_ref[0].astype(jnp.float32),
+        precision=lax.Precision.HIGHEST,
+        preferred_element_type=jnp.float32,
+    )
+
+
+def mix_rows(mixer, stack):
+    held, total_rows, side = stack.shape
+    rows = mixer.shape[0]
+    return pl.pallas_call(
+        mix_kernel,
+        out_shape=jax.ShapeDtypeStruct((held, rows, side), jnp.float32),
+        grid=(held,),
+        in_specs=[
+            pl.BlockSpec((rows, total_rows), lambda v: (0, 0)),
+            pl.BlockSpec((1, total_rows, side), lambda v: (v, 0, 0)),
+        ],
+        out_specs=pl.BlockSpec((1, rows, side), lambda v: (v, 0, 0)),
+        name="mix_rows",
+    )(mixer, stack)
+
+
 def owner_order(nv, count, order):
     per = nv // count
     owners = []
@@ -149,13 +174,12 @@
     return np.concatenate([np.arange(per) + o * per for o in owners])
 
 
-def body(potentials, orbitals, levels, occ_index, coul_rows, coul_cols):
+def program(potentials, orbitals, levels, occ_index, coul_rows, coul_cols):
     nv, points_dev = potentials.shape
     volume = points_dev * lax.axis_size("cell")
     orb_count = lax.axis_size("orb")
     my_rank = lax.axis_index("orb")
     per_orb = orbitals.shape[0]
-    slots = occ_index.shape[0]
     orb_bits = bits_of("orb")
     cell_bits = bits_of("cell")
     orders = [orb_bits, orb_bits[1:] + orb_bits[:1]]
@@ -221,19 +245,29 @@
     owned_sum = jnp.concatenate(owned, 1)
 
     row_count = points_dev // SIDE
-    plane_rows = owned_sum.reshape(owned_sum.shape[0], row_count, SIDE)
-    by_columns = jnp.einsum("vrc,dc->vrd", plane_rows, coul_cols, precision=lax.Precision.HIGHEST)
-    mixed_rows = jnp.einsum(
-        "ab,vbc->vac",
-        coul_rows,
-        lax.all_to_all(by_columns, "cell", split_axis=2, concat_axis=1, tiled=True),
-        precision=lax.Precision.HIGHEST,
-    )
-    return lax.all_to_all(mixed_rows, "cell", split_axis=1, concat_axis=2, tiled=True)
+    held = owned_sum.shape[0]
+    plane = jnp.dot(
+        owned_sum.reshape(held * row_count, SIDE), coul_cols.T, precision=lax.Precision.HIGHEST
+    )
+    stack = plane.astype(jnp.bfloat16).reshape(held, row_count, SIDE)
+    offsets = [0]
+    for bit in cell_bits[::-1]:
+        stack = jnp.concatenate([stack, swap(stack, "cell", bit)], 1)
+        offsets = offsets + [o ^ bit for o in offsets]
+    my_cell = lax.axis_index("cell")
+    my_rows = lax.dynamic_slice_in_dim(coul_rows, my_cell * row_count, row_count, 0)
+    mixer = jnp.concatenate(
+        [
+            lax.dynamic_slice_in_dim(my_rows, (my_cell ^ o) * row_count, row_count, 1)
+            for o in offsets
+        ],
+        1,
+    )
+    return mix_rows(mixer, stack)
 
 
 def solution(mesh):
     placed = (P(None, "cell"), P("orb", "cell"), P(), P(), P(), P())
     return jax.shard_map(
-        body, mesh=mesh, in_specs=placed, out_specs=P("orb", "cell", None), check_vma=False
-    )
+        program, mesh=mesh, in_specs=placed, out_specs=P("orb", "cell", None), check_vma=False
+    )

time: 289 us -> 260 us (0.90)
  blocking collectives: 28.4 us -> 0 us
  local copies, waits for them, and re-layouts: 19.7 us -> 3.28 us
  waiting for transfers between devices: 102 us -> 112 us
  Pallas kernels: 79.5 us -> 88 us
  other arithmetic: 12.1 us -> 8.39 us
    all_to_all x2 -> x0, blocking collectives: 28.4 us -> none  [the longest x1 14.4 us: body(): lax.all_to_all(by_columns, 'cell', split_axis=2, concat_axis=1, tiled=True)]
    ppermute x28 -> x30, waiting for transfers between devices: 102 us -> 112 us  [swap(): return lax.ppermute(x, axis, [(s, s ^ bit) for s in range(n)])]
    all_to_all x5 -> x0, local copies, waits for them, and re-layouts: 10.1 us -> none  [the longest x2 5.14 us: body(): lax.all_to_all(mixed_rows, 'cell', split_axis=1, concat_axis=2, tiled=True)]
    pallas_call x0 -> x1, Pallas kernels: none -> 8.37 us  [mix_rows(): pl.pallas_call(mix_kernel, out_shape=jax.ShapeDtypeStruct((held, rows, si...]
    all_to_all x2 -> x0, other arithmetic: 5.83 us -> none  [the longest x1 2.91 us: body(): lax.all_to_all(mixed_rows, 'cell', split_axis=1, concat_axis=2, tiled=True)]
    unnamed x29 -> x24, local copies, waits for them, and re-layouts: 4.42 us -> 0.42 us
    ppermute x28 -> x30, starting transfers between devices: 38.4 us -> 40 us  [swap(): return lax.ppermute(x, axis, [(s, s ^ bit) for s in range(n)])]
    dot_general x6 -> x5, matrix products: 6.46 us -> 5.65 us  [the longest x2 2.48 us: program(): jnp.dot(place, guess, preferred_element_type=jnp.float32)]
  transfers between devices with their start and end apart: 28 -> 30, of which waited for: 20 -> 22; matrix products, arithmetic and copies ran while one was open for 2% -> 2% of each run, Pallas kernels for 8% -> 9%
where the time goes in v2:
time: 260 us; the launch traced here: 258 us
  waiting for transfers between devices  112 us (43%)
  Pallas kernels  88 us (34%)
  starting transfers between devices  40 us (15%)
  other arithmetic  8.39 us (3%)
  matrix products  5.65 us (2%)
  local copies, waits for them, and re-layouts  3.28 us (1%)
    ppermute x30, waiting for transfers between devices, swap(): return lax.ppermute(x, axis, [(s, s ^ bit) for s in range(n)])  112 us
    pallas_call x2, Pallas kernels, project(): pl.pallas_call(functools.partial(project_kernel, max(1, 256 // stored)),...  44 us
    ppermute x30, starting transfers between devices, swap(): return lax.ppermute(x, axis, [(s, s ^ bit) for s in range(n)])  40 us
    pallas_call x4, Pallas kernels, respond(): pl.pallas_call(functools.partial(respond_kernel, max(1, 256 // stored)),...  35.6 us
    pallas_call x1, Pallas kernels, mix_rows(): pl.pallas_call(mix_kernel, out_shape=jax.ShapeDtypeStruct((held, rows, si...  8.37 us
  transfers between devices with their start and end apart: 30, of which 22 were waited for; matrix products, arithmetic and copies ran while one was open for 2% of the time, Pallas kernels for 9%

profile of v2, /device:TPU:0, one launch (start us, length us, event | category | flops | bytes accessed | tf_op | source)
XLA Modules:
  0.0 258.0 jit_solution(17879464576121131018)
XLA Ops:
  0.0 1.9 convolution_convert_fusion
  2.7 3.1 %collective-permute-start.6 = (bf16[64,4096]{1,0:T(8,128)(2,1)}, bf16[64,4096]{1,0:T(8,128)(2,1)S(1)}, u32[]{:S(2)}, u32[]{:S(2)}) collective-permute-start(bf16[64,4096]{1,0:T(8,128)(2,1)} %constant_dynamic-slice_fusion.5), channel_id=1, source_target_pairs={{0,8},{4,12},{8,0},{12,4},{16,24},{20,28},{24,16},{28,20},{1,9},{5... | collective-permute-start | bytes 1572872 | tf_op jit(solution)/shard_map/ppermute | solution.py:19
  7.1 1.5 collective-permute-start
  8.6 9.3 %collective-permute-done.6 = bf16[64,4096]{1,0:T(8,128)(2,1)S(1)} collective-permute-done((bf16[64,4096]{1,0:T(8,128)(2,1)}, bf16[64,4096]{1,0:T(8,128)(2,1)S(1)}, u32[]{:S(2)}, u32[]{:S(2)}) %collective-permute-start.6) | collective-permute-done | bytes 524320 | tf_op jit(solution)/shard_map/ppermute | solution.py:19
  18.1 2.8 %collective-permute-start.7 = (bf16[64,2048]{1,0:T(8,128)(2,1)S(1)}, bf16[64,2048]{1,0:T(8,128)(2,1)S(1)}, u32[]{:S(2)}, u32[]{:S(2)}) collective-permute-start(bf16[64,2048]{1,0:T(8,128)(2,1)S(1)} %constant_dynamic-slice_fusion.4), channel_id=1, source_target_pairs={{0,16},{4,20},{8,24},{12,28},{16,0},{20,4},{24,8},{28,12},{1,17},{... | collective-permute-start | bytes 786440 | tf_op jit(solution)/shard_map/ppermute | solution.py:19
  21.1 1.6 collective-permute-start.1
  22.7 9.5 %collective-permute-done.7 = bf16[64,2048]{1,0:T(8,128)(2,1)S(1)} collective-permute-done((bf16[64,2048]{1,0:T(8,128)(2,1)S(1)}, bf16[64,2048]{1,0:T(8,128)(2,1)S(1)}, u32[]{:S(2)}, u32[]{:S(2)}) %collective-permute-start.7) | collective-permute-done | bytes 262176 | tf_op jit(solution)/shard_map/ppermute | solution.py:19
  32.4 1.4 collective-permute-start.8
  34.2 3.2 %collective-permute-done.8 = bf16[64,1024]{1,0:T(8,128)(2,1)S(1)} collective-permute-done((bf16[64,1024]{1,0:T(8,128)(2,1)S(1)}, bf16[64,1024]{1,0:T(8,128)(2,1)S(1)}, u32[]{:S(2)}, u32[]{:S(2)}) %collective-permute-start.8) | collective-permute-done | bytes 131104 | tf_op jit(solution)/shard_map/ppermute | solution.py:19
  37.4 1.4 collective-permute-start.9
  38.8 4.6 %collective-permute-done.2 = bf16[64,1024]{1,0:T(8,128)(2,1)S(1)} collective-permute-done((bf16[64,1024]{1,0:T(8,128)(2,1)S(1)}, bf16[64,1024]{1,0:T(8,128)(2,1)S(1)}, u32[]{:S(2)}, u32[]{:S(2)}) %collective-permute-start.2) | collective-permute-done | bytes 131104 | tf_op jit(solution)/shard_map/ppermute | solution.py:19
  43.6 3.0 %collective-permute-start.10 = (bf16[64,2048]{1,0:T(8,128)(2,1)S(1)}, bf16[64,2048]{1,0:T(8,128)(2,1)S(1)}, u32[]{:S(2)}, u32[]{:S(2)}) collective-permute-start(bf16[64,2048]{1,0:T(8,128)(2,1)S(1)} %pad_maximum_fusion.12), channel_id=1, source_target_pairs={{0,16},{4,20},{8,24},{12,28},{16,0},{20,4},{24,8},{28,12},{1,17},{... | collective-permute-start | bytes 786440 | tf_op jit(solution)/shard_map/ppermute | solution.py:19
  46.6 7.6 %collective-permute-done.3 = bf16[64,1024]{1,0:T(8,128)(2,1)S(1)} collective-permute-done((bf16[64,1024]{1,0:T(8,128)(2,1)S(1)}, bf16[64,1024]{1,0:T(8,128)(2,1)S(1)}, u32[]{:S(2)}, u32[]{:S(2)}) %collective-permute-start.3) | collective-permute-done | bytes 131104 | tf_op jit(solution)/shard_map/ppermute | solution.py:19
  54.8 4.4 %collective-permute-done.10 = bf16[64,2048]{1,0:T(8,128)(2,1)S(1)} collective-permute-done((bf16[64,2048]{1,0:T(8,128)(2,1)S(1)}, bf16[64,2048]{1,0:T(8,128)(2,1)S(1)}, u32[]{:S(2)}, u32[]{:S(2)}) %collective-permute-start.10) | collective-permute-done | bytes 262176 | tf_op jit(solution)/shard_map/ppermute | solution.py:19
  59.4 5.4 %collective-permute-done.4 = bf16[64,2048]{1,0:T(8,128)(2,1)S(1)} collective-permute-done((bf16[64,2048]{1,0:T(8,128)(2,1)S(1)}, bf16[64,2048]{1,0:T(8,128)(2,1)S(1)}, u32[]{:S(2)}, u32[]{:S(2)}) %collective-permute-start.4) | collective-permute-done | bytes 262176 | tf_op jit(solution)/shard_map/ppermute | solution.py:19
  65.0 7.1 %collective-permute-done.11 = bf16[64,4096]{1,0:T(8,128)(2,1)S(1)} collective-permute-done((bf16[64,4096]{1,0:T(8,128)(2,1)S(1)}, bf16[64,4096]{1,0:T(8,128)(2,1)S(1)}, u32[]{:S(2)}, u32[]{:S(2)}) %collective-permute-start.11) | collective-permute-done | bytes 524320 | tf_op jit(solution)/shard_map/ppermute | solution.py:19
  73.4 21.9 %project.3 = f32[96,4096]{1,0:T(8,128)} custom-call(bf16[64,8192]{1,0:T(8,128)(2,1)} %pad_maximum_fusion.2.occ_ref, bf16[64,16384]{1,0:T(8,128)(2,1)} %orb_ref.11, bf16[96,16384]{1,0:T(8,128)(2,1)} %pot_ref.3), custom_call_target="tpu_custom_call" | custom-call | flops 19327352832 | bytes 3670016 | tf_op jit(solution)/shard_map/project/pallas_call | solution.py:79
  96.6 22.0 %project.2 = f32[96,4096]{1,0:T(8,128)} custom-call(bf16[64,8192]{1,0:T(8,128)(2,1)} %pad_maximum_fusion.1.occ_ref, bf16[64,16384]{1,0:T(8,128)(2,1)} %orb_ref.11, bf16[96,16384]{1,0:T(8,128)(2,1)} %pot_ref.3), custom_call_target="tpu_custom_call" | custom-call | flops 19327352832 | bytes 3670016 | tf_op jit(solution)/shard_map/project/pallas_call | solution.py:79
  118.6 1.6 add.294
  121.1 1.6 collective-permute-done.12
  122.8 1.7 collective-permute-start.13
  124.8 9.2 %collective-permute-done.13 = f32[96,1024]{1,0:T(8,128)S(1)} collective-permute-done((f32[96,1024]{1,0:T(8,128)S(1)}, f32[96,1024]{1,0:T(8,128)S(1)}, u32[]{:S(2)}, u32[]{:S(2)}) %collective-permute-start.13) | collective-permute-done | bytes 393248 | tf_op jit(solution)/shard_map/ppermute | solution.py:19
  134.0 1.7 collective-permute-start.14
  135.7 4.5 %collective-permute-done.14 = bf16[96,1024]{1,0:T(8,128)(2,1)S(1)} collective-permute-done((bf16[96,1024]{1,0:T(8,128)(2,1)S(1)}, bf16[96,1024]{1,0:T(8,128)(2,1)S(1)}, u32[]{:S(2)}, u32[]{:S(2)}) %collective-permute-start.14) | collective-permute-done | bytes 196640 | tf_op jit(solution)/shard_map/ppermute | solution.py:19
  140.4 1.6 collective-permute-done.15
  142.2 1.2 fusion.guess_ref
  143.5 8.8 %respond.4 = f32[96,4096]{1,0:T(8,128)} custom-call(bf16[96,4096]{1,0:T(8,128)(2,1)} %fusion.guess_ref, bf16[64,8192]{1,0:T(8,128)(2,1)} %pad_maximum_fusion.1.occ_ref, bf16[64,16384]{1,0:T(8,128)(2,1)} %orb_ref.11), custom_call_target="tpu_custom_call" | custom-call | flops 9663676416 | bytes 2621440 | tf_op jit(solution)/shard_map/respond/pallas_call | solution.py:120
  152.3 8.9 %respond.6 = f32[96,4096]{1,0:T(8,128)} custom-call(bf16[96,4096]{1,0:T(8,128)(2,1)} %fusion.guess_ref, bf16[64,8192]{1,0:T(8,128)(2,1)} %pad_maximum_fusion.2.occ_ref, bf16[64,16384]{1,0:T(8,128)(2,1)} %orb_ref.11), custom_call_target="tpu_custom_call" | custom-call | flops 9663676416 | bytes 2621440 | tf_op jit(solution)/shard_map/respond/pallas_call | solution.py:120
  162.5 8.9 %respond.5 = f32[96,4096]{1,0:T(8,128)} custom-call(bf16[96,4096]{1,0:T(8,128)(2,1)} %fusion.1.guess_ref, bf16[64,8192]{1,0:T(8,128)(2,1)} %pad_maximum_fusion.1.occ_ref, bf16[64,16384]{1,0:T(8,128)(2,1)} %orb_ref.11), custom_call_target="tpu_custom_call" | custom-call | flops 9663676416 | bytes 2621440 | tf_op jit(solution)/shard_map/respond/pallas_call | solution.py:120
  171.3 9.0 %respond.7 = f32[96,4096]{1,0:T(8,128)} custom-call(bf16[96,4096]{1,0:T(8,128)(2,1)} %fusion.1.guess_ref, bf16[64,8192]{1,0:T(8,128)(2,1)} %pad_maximum_fusion.2.occ_ref, bf16[64,16384]{1,0:T(8,128)(2,1)} %orb_ref.11), custom_call_target="tpu_custom_call" | custom-call | flops 9663676416 | bytes 2621440 | tf_op jit(solution)/shard_map/respond/pallas_call | solution.py:120
  180.4 3.4 %collective-permute-start.16 = (bf16[48,4096]{1,0:T(8,128)(2,1)S(1)}, bf16[48,4096]{1,0:T(8,128)(2,1)S(1)}, u32[]{:S(2)}, u32[]{:S(2)}) collective-permute-start(bf16[48,4096]{1,0:T(8,128)(2,1)S(1)} %dynamic-slice_convert_fusion.3), channel_id=1, source_target_pairs={{0,4},{4,0},{8,12},{12,8},{16,20},{20,16},{24,28},{28,24},{1,5},{5... | collective-permute-start | bytes 1179656 | tf_op jit(solution)/shard_map/ppermute | solution.py:19
  184.1 2.1 collective-permute-start.25
  186.2 7.6 %collective-permute-done.16 = bf16[48,4096]{1,0:T(8,128)(2,1)S(1)} collective-permute-done((bf16[48,4096]{1,0:T(8,128)(2,1)S(1)}, bf16[48,4096]{1,0:T(8,128)(2,1)S(1)}, u32[]{:S(2)}, u32[]{:S(2)}) %collective-permute-start.16) | collective-permute-done | bytes 393248 | tf_op jit(solution)/shard_map/ppermute | solution.py:19
  193.9 1.9 collective-permute-done.19
  196.0 3.6 %collective-permute-start.20 = (bf16[24,4096]{1,0:T(8,128)(2,1)S(1)}, bf16[24,4096]{1,0:T(8,128)(2,1)S(1)}, u32[]{:S(2)}, u32[]{:S(2)}) collective-permute-start(bf16[24,4096]{1,0:T(8,128)(2,1)S(1)} %dynamic-slice_convert_fusion.6), channel_id=1, source_target_pairs={{0,16},{4,20},{8,24},{12,28},{16,0},{20,4},{24,8},{28,12},{1,17},{... | collective-permute-start | bytes 589832 | tf_op jit(solution)/shard_map/ppermute | solution.py:19
  199.6 2.0 collective-permute-done.22
  201.8 6.7 %collective-permute-done.25 = bf16[48,4096]{1,0:T(8,128)(2,1)S(1)} collective-permute-done((bf16[48,4096]{1,0:T(8,128)(2,1)S(1)}, bf16[48,4096]{1,0:T(8,128)(2,1)S(1)}, u32[]{:S(2)}, u32[]{:S(2)}) %collective-permute-start.25) | collective-permute-done | bytes 393248 | tf_op jit(solution)/shard_map/ppermute | solution.py:19
  208.6 3.1 %collective-permute-start.26 = (bf16[24,4096]{1,0:T(8,128)(2,1)S(1)}, bf16[24,4096]{1,0:T(8,128)(2,1)S(1)}, u32[]{:S(2)}, u32[]{:S(2)}) collective-permute-start(bf16[24,4096]{1,0:T(8,128)(2,1)S(1)} %dynamic-slice_convert_fusion.4), channel_id=1, source_target_pairs={{0,16},{4,20},{8,24},{12,28},{16,0},{20,4},{24,8},{28,12},{1,17},{... | collective-permute-start | bytes 589832 | tf_op jit(solution)/shard_map/ppermute | solution.py:19
  211.7 1.6 collective-permute-done.17
  213.4 5.0 %collective-permute-start.18 = (bf16[12,4096]{1,0:T(8,128)(2,1)S(1)}, bf16[12,4096]{1,0:T(8,128)(2,1)S(1)}, u32[]{:S(2)}, u32[]{:S(2)}) collective-permute-start(bf16[12,4096]{1,0:T(8,128)(2,1)S(1)} %dynamic-slice_convert_fusion.11), channel_id=1, source_target_pairs={{0,16},{4,20},{8,24},{12,28},{16,0},{20,4},{24,8},{28,12},{1,17},{... | collective-permute-start | bytes 294920 | tf_op jit(solution)/shard_map/ppermute | solution.py:19
  218.6 2.0 collective-permute-done.23
  222.0 9.8 %collective-permute-done.18 = bf16[12,4096]{1,0:T(8,128)(2,1)S(1)} collective-permute-done((bf16[12,4096]{1,0:T(8,128)(2,1)S(1)}, bf16[12,4096]{1,0:T(8,128)(2,1)S(1)}, u32[]{:S(2)}, u32[]{:S(2)}) %collective-permute-start.18) | collective-permute-done | bytes 98336 | tf_op jit(solution)/shard_map/ppermute | solution.py:19
  231.9 2.2 collective-permute-done.24
  235.3 1.8 collective-permute-start.28
  237.1 8.8 %collective-permute-done.28 = bf16[12,64,256]{2,1,0:T(8,128)(2,1)S(1)} collective-permute-done((bf16[12,64,256]{2,1,0:T(8,128)(2,1)S(1)}, bf16[12,64,256]{2,1,0:T(8,128)(2,1)S(1)}, u32[]{:S(2)}, u32[]{:S(2)}) %collective-permute-start.28) | collective-permute-done | bytes 393248 | tf_op jit(solution)/shard_map/ppermute | solution.py:19
  247.0 1.4 collective-permute-done.29
  248.4 1.3 pad_maximum_fusion.stack_ref
  249.6 8.4 %mix_rows.1 = f32[12,64,256]{2,1,0:T(8,128)} custom-call(f32[64,256]{1,0:T(8,128)} %pad_maximum_fusion.13.mixer_ref, bf16[12,256,256]{2,1,0:T(8,128)(2,1)} %pad_maximum_fusion.stack_ref), custom_call_target="tpu_custom_call" | custom-call | tf_op jit(solution)/shard_map/mix_rows/pallas_call | solution.py:152
  (119 shorter events, 14.3 us)
Async XLA Ops:
  0.0 234.5 %copy-start = (f32[256,256]{1,0:T(8,128)S(1)}, f32[256,256]{1,0:T(8,128)}, u32[]{:S(2)}) copy-start(f32[256,256]{1,0:T(8,128)} %param.13) | copy-start | bytes 786436
  0.0 5.8 %copy-start.1 = (bf16[64,16384]{1,0:T(8,128)(2,1)S(1)}, bf16[64,16384]{1,0:T(8,128)(2,1)}, u32[]{:S(2)}) copy-start(bf16[64,16384]{1,0:T(8,128)(2,1)} %orb_ref.11) | copy-start | bytes 6291460
  0.0 5.8 %copy-start.10 = (s32[64]{0:T(128)S(1)}, s32[64]{0:T(128)}, u32[]{:S(2)}) copy-start(s32[64]{0:T(128)} %param.11) | copy-start | bytes 772
  2.7 15.2 %collective-permute-start.6 = (bf16[64,4096]{1,0:T(8,128)(2,1)}, bf16[64,4096]{1,0:T(8,128)(2,1)S(1)}, u32[]{:S(2)}, u32[]{:S(2)}) collective-permute-start(bf16[64,4096]{1,0:T(8,128)(2,1)} %constant_dynamic-slice_fusion.5), channel_id=1, source_target_pairs={{0,8},{4,12},{8,0},{12,4},{16,24},{20,28},{24,16},{28,20},{1,9},{5... | collective-permute-start | bytes 1572872 | tf_op jit(solution)/shard_map/ppermute | solution.py:19
  7.1 13.8 %collective-permute-start = (bf16[64,4096]{1,0:T(8,128)(2,1)}, bf16[64,4096]{1,0:T(8,128)(2,1)S(1)}, u32[]{:S(2)}, u32[]{:S(2)}) collective-permute-start(bf16[64,4096]{1,0:T(8,128)(2,1)} %constant_dynamic-slice_fusion.8), channel_id=1, source_target_pairs={{0,4},{4,0},{8,12},{12,8},{16,20},{20,16},{24,28},{28,24},{1,5},{5... | collective-permute-start | bytes 1572872 | tf_op jit(solution)/shard_map/ppermute | solution.py:19
  18.1 14.2 %collective-permute-start.7 = (bf16[64,2048]{1,0:T(8,128)(2,1)S(1)}, bf16[64,2048]{1,0:T(8,128)(2,1)S(1)}, u32[]{:S(2)}, u32[]{:S(2)}) collective-permute-start(bf16[64,2048]{1,0:T(8,128)(2,1)S(1)} %constant_dynamic-slice_fusion.4), channel_id=1, source_target_pairs={{0,16},{4,20},{8,24},{12,28},{16,0},{20,4},{24,8},{28,12},{1,17},{... | collective-permute-start | bytes 786440 | tf_op jit(solution)/shard_map/ppermute | solution.py:19
  21.1 12.7 %collective-permute-start.1 = (bf16[64,2048]{1,0:T(8,128)(2,1)S(1)}, bf16[64,2048]{1,0:T(8,128)(2,1)S(1)}, u32[]{:S(2)}, u32[]{:S(2)}) collective-permute-start(bf16[64,2048]{1,0:T(8,128)(2,1)S(1)} %constant_dynamic-slice_fusion.7), channel_id=1, source_target_pairs={{0,8},{4,12},{8,0},{12,4},{16,24},{20,28},{24,16},{28,20},{1,9},{5... | collective-permute-start | bytes 786440 | tf_op jit(solution)/shard_map/ppermute | solution.py:19
  32.4 5.0 %collective-permute-start.8 = (bf16[64,1024]{1,0:T(8,128)(2,1)S(1)}, bf16[64,1024]{1,0:T(8,128)(2,1)S(1)}, u32[]{:S(2)}, u32[]{:S(2)}) collective-permute-start(bf16[64,1024]{1,0:T(8,128)(2,1)S(1)} %constant_dynamic-slice_fusion.3), channel_id=1, source_target_pairs={{0,4},{4,0},{8,12},{12,8},{16,20},{20,16},{24,28},{28,24},{1,5},{5... | collective-permute-start | bytes 393224 | tf_op jit(solution)/shard_map/ppermute | solution.py:19
  33.9 9.5 %collective-permute-start.2 = (bf16[64,1024]{1,0:T(8,128)(2,1)S(1)}, bf16[64,1024]{1,0:T(8,128)(2,1)S(1)}, u32[]{:S(2)}, u32[]{:S(2)}) collective-permute-start(bf16[64,1024]{1,0:T(8,128)(2,1)S(1)} %constant_dynamic-slice_fusion.6), channel_id=1, source_target_pairs={{0,16},{4,20},{8,24},{12,28},{16,0},{20,4},{24,8},{28,12},{1,17},{... | collective-permute-start | bytes 393224 | tf_op jit(solution)/shard_map/ppermute | solution.py:19
  37.4 6.1 %collective-permute-start.9 = (bf16[64,1024]{1,0:T(8,128)(2,1)S(1)}, bf16[64,1024]{1,0:T(8,128)(2,1)S(1)}, u32[]{:S(2)}, u32[]{:S(2)}) collective-permute-start(bf16[64,1024]{1,0:T(8,128)(2,1)S(1)} %dynamic-slice_add_fusion.5), channel_id=1, source_target_pairs={{0,4},{4,0},{8,12},{12,8},{16,20},{20,16},{24,28},{28,24},{1,5},{5... | collective-permute-start | bytes 393224 | tf_op jit(solution)/shard_map/ppermute | solution.py:19
  43.5 10.7 %collective-permute-start.3 = (bf16[64,1024]{1,0:T(8,128)(2,1)S(1)}, bf16[64,1024]{1,0:T(8,128)(2,1)S(1)}, u32[]{:S(2)}, u32[]{:S(2)}) collective-permute-start(bf16[64,1024]{1,0:T(8,128)(2,1)S(1)} %dynamic-slice_add_fusion.6), channel_id=1, source_target_pairs={{0,16},{4,20},{8,24},{12,28},{16,0},{20,4},{24,8},{28,12},{1,17},{... | collective-permute-start | bytes 393224 | tf_op jit(solution)/shard_map/ppermute | solution.py:19
  43.6 15.6 %collective-permute-start.10 = (bf16[64,2048]{1,0:T(8,128)(2,1)S(1)}, bf16[64,2048]{1,0:T(8,128)(2,1)S(1)}, u32[]{:S(2)}, u32[]{:S(2)}) collective-permute-start(bf16[64,2048]{1,0:T(8,128)(2,1)S(1)} %pad_maximum_fusion.12), channel_id=1, source_target_pairs={{0,16},{4,20},{8,24},{12,28},{16,0},{20,4},{24,8},{28,12},{1,17},{... | collective-permute-start | bytes 786440 | tf_op jit(solution)/shard_map/ppermute | solution.py:19
  54.3 10.5 %collective-permute-start.4 = (bf16[64,2048]{1,0:T(8,128)(2,1)S(1)}, bf16[64,2048]{1,0:T(8,128)(2,1)S(1)}, u32[]{:S(2)}, u32[]{:S(2)}) collective-permute-start(bf16[64,2048]{1,0:T(8,128)(2,1)S(1)} %pad_maximum_fusion.11), channel_id=1, source_target_pairs={{0,8},{4,12},{8,0},{12,4},{16,24},{20,28},{24,16},{28,20},{1,9},{5... | collective-permute-start | bytes 786440 | tf_op jit(solution)/shard_map/ppermute | solution.py:19
  59.3 12.8 %collective-permute-start.11 = (bf16[64,4096]{1,0:T(8,128)(2,1)S(1)}, bf16[64,4096]{1,0:T(8,128)(2,1)S(1)}, u32[]{:S(2)}, u32[]{:S(2)}) collective-permute-start(bf16[64,4096]{1,0:T(8,128)(2,1)S(1)} %pad_maximum_fusion.7), channel_id=1, source_target_pairs={{0,8},{4,12},{8,0},{12,4},{16,24},{20,28},{24,16},{28,20},{1,9},{5... | collective-permute-start | bytes 1572872 | tf_op jit(solution)/shard_map/ppermute | solution.py:19
  64.9 30.4 %collective-permute-start.5 = (bf16[64,4096]{1,0:T(8,128)(2,1)S(1)}, bf16[64,4096]{1,0:T(8,128)(2,1)S(1)}, u32[]{:S(2)}, u32[]{:S(2)}) collective-permute-start(bf16[64,4096]{1,0:T(8,128)(2,1)S(1)} %pad_maximum_fusion.6), channel_id=1, source_target_pairs={{0,4},{4,0},{8,12},{12,8},{16,20},{20,16},{24,28},{28,24},{1,5},{5... | collective-permute-start | bytes 1572872 | tf_op jit(solution)/shard_map/ppermute | solution.py:19
  96.6 22.0 %copy-start.2 = (f32[96,4096]{1,0:T(8,128)S(1)}, f32[96,4096]{1,0:T(8,128)}, u32[]{:S(2)}) copy-start(f32[96,4096]{1,0:T(8,128)} %project.3) | copy-start | bytes 4718596
  120.2 0.7 copy-start.11
  120.3 2.4 collective-permute-start.12
  122.8 11.2 %collective-permute-start.13 = (f32[96,1024]{1,0:T(8,128)S(1)}, f32[96,1024]{1,0:T(8,128)S(1)}, u32[]{:S(2)}, u32[]{:S(2)}) collective-permute-start(f32[96,1024]{1,0:T(8,128)S(1)} %constant_dynamic-slice_fusion.1), channel_id=1, source_target_pairs={{0,2},{1,3},{2,0},{3,1},{4,6},{5,7},{6,4},{7,5},{8,10},{9,11},{10,... | collective-permute-start | bytes 1179656 | tf_op jit(solution)/shard_map/ppermute | solution.py:19
  134.0 6.2 %collective-permute-start.14 = (bf16[96,1024]{1,0:T(8,128)(2,1)S(1)}, bf16[96,1024]{1,0:T(8,128)(2,1)S(1)}, u32[]{:S(2)}, u32[]{:S(2)}) collective-permute-start(bf16[96,1024]{1,0:T(8,128)(2,1)S(1)} %multiply_convert_fusion), channel_id=1, source_target_pairs={{0,2},{1,3},{2,0},{3,1},{4,6},{5,7},{6,4},{7,5},{8,10},{9,11},{10,... | collective-permute-start | bytes 589832 | tf_op jit(solution)/shard_map/ppermute | solution.py:19
  135.7 6.5 %copy-start.9 = (bf16[96,96]{1,0:T(8,128)(2,1)S(1)}, bf16[96,96]{1,0:T(8,128)(2,1)}, u32[]{:S(2)}) copy-start(bf16[96,96]{1,0:T(8,128)(2,1)} %constant.272.clone) | copy-start | bytes 55300
  140.3 1.8 collective-permute-start.15
  152.3 8.9 %copy-start.8 = (bf16[96,96]{1,0:T(8,128)(2,1)S(1)}, bf16[96,96]{1,0:T(8,128)(2,1)}, u32[]{:S(2)}) copy-start(bf16[96,96]{1,0:T(8,128)(2,1)} %constant.273.clone) | copy-start | bytes 55300
  171.3 9.0 %copy-start.6 = (f32[96,4096]{1,0:T(8,128)S(1)}, f32[96,4096]{1,0:T(8,128)}, u32[]{:S(2)}) copy-start(f32[96,4096]{1,0:T(8,128)} %respond.4) | copy-start | bytes 4718596
  171.3 12.5 %copy-start.5 = (f32[96,4096]{1,0:T(8,128)S(1)}, f32[96,4096]{1,0:T(8,128)}, u32[]{:S(2)}) copy-start(f32[96,4096]{1,0:T(8,128)} %respond.5) | copy-start | bytes 4718596
  171.3 12.6 %copy-start.4 = (f32[96,4096]{1,0:T(8,128)S(1)}, f32[96,4096]{1,0:T(8,128)}, u32[]{:S(2)}) copy-start(f32[96,4096]{1,0:T(8,128)} %respond.6) | copy-start | bytes 4718596
  180.4 3.7 %copy-start.3 = (f32[96,4096]{1,0:T(8,128)S(1)}, f32[96,4096]{1,0:T(8,128)}, u32[]{:S(2)}) copy-start(f32[96,4096]{1,0:T(8,128)} %respond.7) | copy-start | bytes 4718596
  180.4 13.3 %collective-permute-start.16 = (bf16[48,4096]{1,0:T(8,128)(2,1)S(1)}, bf16[48,4096]{1,0:T(8,128)(2,1)S(1)}, u32[]{:S(2)}, u32[]{:S(2)}) collective-permute-start(bf16[48,4096]{1,0:T(8,128)(2,1)S(1)} %dynamic-slice_convert_fusion.3), channel_id=1, source_target_pairs={{0,4},{4,0},{8,12},{12,8},{16,20},{20,16},{24,28},{28,24},{1,5},{5... | collective-permute-start | bytes 1179656 | tf_op jit(solution)/shard_map/ppermute | solution.py:19
  183.8 12.1 %collective-permute-start.19 = (bf16[48,4096]{1,0:T(8,128)(2,1)S(1)}, bf16[48,4096]{1,0:T(8,128)(2,1)S(1)}, u32[]{:S(2)}, u32[]{:S(2)}) collective-permute-start(bf16[48,4096]{1,0:T(8,128)(2,1)S(1)} %dynamic-slice_convert_fusion.2), channel_id=1, source_target_pairs={{0,8},{4,12},{8,0},{12,4},{16,24},{20,28},{24,16},{28,20},{1,9},{5... | collective-permute-start | bytes 1179656 | tf_op jit(solution)/shard_map/ppermute | solution.py:19
  184.0 17.6 %collective-permute-start.22 = (bf16[48,4096]{1,0:T(8,128)(2,1)S(1)}, bf16[48,4096]{1,0:T(8,128)(2,1)S(1)}, u32[]{:S(2)}, u32[]{:S(2)}) collective-permute-start(bf16[48,4096]{1,0:T(8,128)(2,1)S(1)} %dynamic-slice_convert_fusion.1), channel_id=1, source_target_pairs={{0,4},{4,0},{8,12},{12,8},{16,20},{20,16},{24,28},{28,24},{1,5},{5... | collective-permute-start | bytes 1179656 | tf_op jit(solution)/shard_map/ppermute | solution.py:19
  184.1 24.4 %collective-permute-start.25 = (bf16[48,4096]{1,0:T(8,128)(2,1)S(1)}, bf16[48,4096]{1,0:T(8,128)(2,1)S(1)}, u32[]{:S(2)}, u32[]{:S(2)}) collective-permute-start(bf16[48,4096]{1,0:T(8,128)(2,1)S(1)} %dynamic-slice_convert_fusion), channel_id=1, source_target_pairs={{0,8},{4,12},{8,0},{12,4},{16,24},{20,28},{24,16},{28,20},{1,9},{5... | collective-permute-start | bytes 1179656 | tf_op jit(solution)/shard_map/ppermute | solution.py:19
  193.9 19.5 %collective-permute-start.17 = (bf16[24,4096]{1,0:T(8,128)(2,1)S(1)}, bf16[24,4096]{1,0:T(8,128)(2,1)S(1)}, u32[]{:S(2)}, u32[]{:S(2)}) collective-permute-start(bf16[24,4096]{1,0:T(8,128)(2,1)S(1)} %dynamic-slice_convert_fusion.7), channel_id=1, source_target_pairs={{0,8},{4,12},{8,0},{12,4},{16,24},{20,28},{24,16},{28,20},{1,9},{5... | collective-permute-start | bytes 589832 | tf_op jit(solution)/shard_map/ppermute | solution.py:19
  196.0 22.4 %collective-permute-start.20 = (bf16[24,4096]{1,0:T(8,128)(2,1)S(1)}, bf16[24,4096]{1,0:T(8,128)(2,1)S(1)}, u32[]{:S(2)}, u32[]{:S(2)}) collective-permute-start(bf16[24,4096]{1,0:T(8,128)(2,1)S(1)} %dynamic-slice_convert_fusion.6), channel_id=1, source_target_pairs={{0,16},{4,20},{8,24},{12,28},{16,0},{20,4},{24,8},{28,12},{1,17},{... | collective-permute-start | bytes 589832 | tf_op jit(solution)/shard_map/ppermute | solution.py:19
  201.7 18.9 %collective-permute-start.23 = (bf16[24,4096]{1,0:T(8,128)(2,1)S(1)}, bf16[24,4096]{1,0:T(8,128)(2,1)S(1)}, u32[]{:S(2)}, u32[]{:S(2)}) collective-permute-start(bf16[24,4096]{1,0:T(8,128)(2,1)S(1)} %dynamic-slice_convert_fusion.5), channel_id=1, source_target_pairs={{0,8},{4,12},{8,0},{12,4},{16,24},{20,28},{24,16},{28,20},{1,9},{5... | collective-permute-start | bytes 589832 | tf_op jit(solution)/shard_map/ppermute | solution.py:19
  208.6 12.9 %collective-permute-start.26 = (bf16[24,4096]{1,0:T(8,128)(2,1)S(1)}, bf16[24,4096]{1,0:T(8,128)(2,1)S(1)}, u32[]{:S(2)}, u32[]{:S(2)}) collective-permute-start(bf16[24,4096]{1,0:T(8,128)(2,1)S(1)} %dynamic-slice_convert_fusion.4), channel_id=1, source_target_pairs={{0,16},{4,20},{8,24},{12,28},{16,0},{20,4},{24,8},{28,12},{1,17},{... | collective-permute-start | bytes 589832 | tf_op jit(solution)/shard_map/ppermute | solution.py:19
  213.4 18.4 %collective-permute-start.18 = (bf16[12,4096]{1,0:T(8,128)(2,1)S(1)}, bf16[12,4096]{1,0:T(8,128)(2,1)S(1)}, u32[]{:S(2)}, u32[]{:S(2)}) collective-permute-start(bf16[12,4096]{1,0:T(8,128)(2,1)S(1)} %dynamic-slice_convert_fusion.11), channel_id=1, source_target_pairs={{0,16},{4,20},{8,24},{12,28},{16,0},{20,4},{24,8},{28,12},{1,17},{... | collective-permute-start | bytes 294920 | tf_op jit(solution)/shard_map/ppermute | solution.py:19
  218.5 15.5 %collective-permute-start.21 = (bf16[12,4096]{1,0:T(8,128)(2,1)S(1)}, bf16[12,4096]{1,0:T(8,128)(2,1)S(1)}, u32[]{:S(2)}, u32[]{:S(2)}) collective-permute-start(bf16[12,4096]{1,0:T(8,128)(2,1)S(1)} %dynamic-slice_convert_fusion.10), channel_id=1, source_target_pairs={{0,4},{4,0},{8,12},{12,8},{16,20},{20,16},{24,28},{28,24},{1,5},{5... | collective-permute-start | bytes 294920 | tf_op jit(solution)/shard_map/ppermute | solution.py:19
  220.7 13.3 %collective-permute-start.24 = (bf16[12,4096]{1,0:T(8,128)(2,1)S(1)}, bf16[12,4096]{1,0:T(8,128)(2,1)S(1)}, u32[]{:S(2)}, u32[]{:S(2)}) collective-permute-start(bf16[12,4096]{1,0:T(8,128)(2,1)S(1)} %dynamic-slice_convert_fusion.9), channel_id=1, source_target_pairs={{0,16},{4,20},{8,24},{12,28},{16,0},{20,4},{24,8},{28,12},{1,17},{... | collective-permute-start | bytes 294920 | tf_op jit(solution)/shard_map/ppermute | solution.py:19
  221.6 12.5 %collective-permute-start.27 = (bf16[12,4096]{1,0:T(8,128)(2,1)S(1)}, bf16[12,4096]{1,0:T(8,128)(2,1)S(1)}, u32[]{:S(2)}, u32[]{:S(2)}) collective-permute-start(bf16[12,4096]{1,0:T(8,128)(2,1)S(1)} %dynamic-slice_convert_fusion.8), channel_id=1, source_target_pairs={{0,4},{4,0},{8,12},{12,8},{16,20},{20,16},{24,28},{28,24},{1,5},{5... | collective-permute-start | bytes 294920 | tf_op jit(solution)/shard_map/ppermute | solution.py:19
  234.5 11.6 %copy-start.7 = (f32[256,256]{1,0:T(8,128)S(1)}, f32[256,256]{1,0:T(8,128)}, u32[]{:S(2)}) copy-start(f32[256,256]{1,0:T(8,128)} %param.12) | copy-start | bytes 786436
  235.3 10.6 %collective-permute-start.28 = (bf16[12,64,256]{2,1,0:T(8,128)(2,1)S(1)}, bf16[12,64,256]{2,1,0:T(8,128)(2,1)S(1)}, u32[]{:S(2)}, u32[]{:S(2)}) collective-permute-start(bf16[12,64,256]{2,1,0:T(8,128)(2,1)S(1)} %bitcast.10), channel_id=1, source_target_pairs={{0,2},{1,3},{2,0},{3,1},{4,6},{5,7},{6,4},{7,5},{8,10},{9,11},{10,... | collective-permute-start | bytes 1179656 | tf_op jit(solution)/shard_map/ppermute | solution.py:19
  246.0 2.4 collective-permute-start.29

commit v3 on v2

--- a/solution.py
+++ b/solution.py
@@ -9,7 +9,7 @@
 from jax.sharding import PartitionSpec as P
 
 SIDE = 256
-GATHER_CHUNKS = 2
+MESH = pl.DeviceIdType.MESH
 RESPONSE_CHUNKS = 4
 VMEM = 56 * 1024 * 1024
 
@@ -48,53 +48,143 @@
     return jnp.concatenate([occ_ref[i : i + 1, :] * orb for i in range(first, first + count)], 0)
 
 
-def project_kernel(group, occ_ref, orb_ref, pot_ref, out_ref, acc):
-    step = pl.program_id(0)
-
-    @pl.when(step == 0)
-    def _():
-        acc[...] = jnp.zeros_like(acc)
-
-    turned = pot_ref[...].T
-    orb = orb_ref[...]
+def partner_of(axis, bit):
+    me = lax.axis_index(axis)
+    return me + bit - 2 * bit * ((me // bit) % 2)
+
+
+def greet(axis, bits):
+    barrier = pltpu.get_barrier_semaphore()
+    for bit in bits:
+        pl.semaphore_signal(
+            barrier, inc=1, device_id={axis: partner_of(axis, bit)}, device_id_type=MESH
+        )
+    pl.semaphore_wait(barrier, len(bits))
+
+
+def project_block(group, at, block, occ_ref, orb_ref, pot_ref, acc):
+    turned = pot_ref[:, pl.ds(at, block)].T
+    orb = orb_ref[:, pl.ds(at, block)]
     rows = group * orb.shape[0]
     for k in range(occ_ref.shape[0] // group):
-        pairs = pair_rows(occ_ref, orb, k * group, group)
+        pairs = jnp.concatenate(
+            [
+                occ_ref[i : i + 1, pl.ds(at, block)] * orb
+                for i in range(k * group, (k + 1) * group)
+            ],
+            0,
+        )
         acc[k * rows : (k + 1) * rows, :] += jnp.dot(
             pairs, turned, preferred_element_type=jnp.float32
         )
 
-    @pl.when(step == pl.num_programs(0) - 1)
-    def _():
-        out_ref[...] = acc[...].T
-
-
-def project(occ, orbitals, potentials, start):
-    slots, width = occ.shape
-    stored = orbitals.shape[0]
+
+def gather_kernel(bits, chunks, group, picker, orb, pot, occ, inter, work, land, acc, sent, came):
+    points = orb.shape[1]
+    chunk = points // chunks
+    depth = len(bits)
+    block = min(1024, chunk)
+    orders = [bits, bits[1:] + bits[:1]]
+    place = [c * chunk for c in range(chunks)]
+    flying = [None] * chunks
+
+    def push(c, step, src, dst, bit):
+        copy = pltpu.make_async_remote_copy(
+            src_ref=src,
+            dst_ref=dst,
+            send_sem=sent.at[c, step],
+            recv_sem=came.at[c, step],
+            device_id={"orb": partner_of("orb", bit)},
+            device_id_type=MESH,
+        )
+        copy.start()
+        flying[c] = copy
+
+    def advance(c, step):
+        order = orders[c % 2]
+        if step == 0:
+            span = slice(c * chunk, (c + 1) * chunk)
+            work[:, span] = jnp.dot(
+                picker[...], orb[:, span], preferred_element_type=jnp.float32
+            ).astype(work.dtype)
+        else:
+            flying[c].wait()
+            if step <= depth:
+                size = chunk >> step
+                here = pl.ds(pl.multiple_of(place[c], 128), size)
+                base = c * chunk + chunk - (chunk >> (step - 1))
+                total = work[:, here] + land[:, base : base + size]
+                if step < depth:
+                    work[:, here] = total
+                else:
+                    occ[:, here] = total
+            else:
+                size = chunk >> (2 * depth - step + 1)
+                bit = order[2 * depth - step]
+                place[c] = place[c] - upper("orb", bit) * size
+        if step < depth:
+            bit = order[step]
+            half = chunk >> (step + 1)
+            side = upper("orb", bit)
+            away = pl.multiple_of(place[c] + (1 - side) * half, 128)
+            base = c * chunk + chunk - (chunk >> step)
+            push(c, step, work.at[:, pl.ds(away, half)], land.at[:, pl.ds(base, half)], bit)
+            place[c] = place[c] + side * half
+        elif step < 2 * depth:
+            size = chunk >> (2 * depth - step)
+            here = pl.ds(pl.multiple_of(place[c], 128), size)
+            push(c, step, occ.at[:, here], occ.at[:, here], order[2 * depth - 1 - step])
+
+    acc[...] = jnp.zeros_like(acc)
+    greet("orb", bits)
+    teams = [list(range(t, min(t + 2, chunks))) for t in range(0, chunks, 2)]
+    for tick in range(2 * depth + len(teams)):
+        for t, team in enumerate(teams):
+            step = tick - t
+            if 0 <= step <= 2 * depth:
+                for c in team:
+                    advance(c, step)
+        done = tick - 2 * depth
+        if 0 <= done < len(teams):
+            team = teams[done]
+            first = team[0] * chunk // block
+
+            @pl.loop(first, first + len(team) * chunk // block)
+            def _(b):
+                at = pl.multiple_of(b * block, block)
+                project_block(group, at, block, occ, orb, pot, acc)
+
+    inter[...] = acc[...].T
+
+
+def gather_project(picker, orbitals, potentials):
+    stored, points = orbitals.shape
+    slots = picker.shape[0]
     nv = potentials.shape[0]
-    block = min(1024, width)
-    shift = start // block
     pairs = slots * stored
+    bits = bits_of("orb")
+    chunks = max(1, min(8, points // (128 << len(bits))))
+    steps = 2 * len(bits)
     return pl.pallas_call(
-        functools.partial(project_kernel, max(1, 256 // stored)),
-        out_shape=jax.ShapeDtypeStruct((nv, pairs), jnp.float32),
-        grid=(width // block,),
-        in_specs=[
-            pl.BlockSpec((slots, block), lambda s: (0, s)),
-            pl.BlockSpec((stored, block), lambda s: (0, s + shift)),
-            pl.BlockSpec((nv, block), lambda s: (0, s + shift)),
+        functools.partial(gather_kernel, bits, chunks, max(1, 256 // stored)),
+        out_shape=(
+            jax.ShapeDtypeStruct((slots, points), jnp.bfloat16),
+            jax.ShapeDtypeStruct((nv, pairs), jnp.float32),
+        ),
+        in_specs=[pl.BlockSpec(memory_space=pltpu.VMEM)] * 3,
+        out_specs=(pl.BlockSpec(memory_space=pltpu.VMEM),) * 2,
+        scratch_shapes=[
+            pltpu.VMEM((slots, points), jnp.bfloat16),
+            pltpu.VMEM((slots, points), jnp.bfloat16),
+            pltpu.VMEM((pairs, nv), jnp.float32),
+            pltpu.SemaphoreType.DMA((chunks, steps)),
+            pltpu.SemaphoreType.DMA((chunks, steps)),
         ],
-        out_specs=pl.BlockSpec((nv, pairs), lambda s: (0, 0)),
-        scratch_shapes=[pltpu.VMEM((pairs, nv), jnp.float32)],
-        compiler_params=pltpu.CompilerParams(vmem_limit_bytes=VMEM),
-        cost_estimate=pl.CostEstimate(
-            flops=2 * pairs * nv * width * 3,
-            bytes_accessed=2 * width * (slots + stored + nv),
-            transcendentals=0,
+        compiler_params=pltpu.CompilerParams(
+            vmem_limit_bytes=VMEM, collective_id=0, has_side_effects=True
         ),
-        name="project",
-    )(occ, orbitals, potentials)
+        name="gather_project",
+    )(picker, orbitals, potentials)
 
 
 def respond_kernel(group, guess_ref, occ_ref, orb_ref, out_ref):
@@ -197,25 +287,7 @@
     owned_ids = my_rank * per_orb + jnp.arange(per_orb, dtype=jnp.int32)
     picker = (occ_index[:, None] == owned_ids[None, :]).astype(jnp.bfloat16)
 
-    chunk = points_dev // GATHER_CHUNKS
-    occ_parts = []
-    for g in range(GATHER_CHUNKS):
-        piece = jnp.dot(
-            picker,
-            orbitals[:, g * chunk : (g + 1) * chunk],
-            preferred_element_type=jnp.float32,
-        ).astype(jnp.bfloat16)
-        order = orders[g % 2]
-        for bit in order:
-            piece = halve(piece, "orb", bit, 1)
-        for bit in order[::-1]:
-            piece = double(piece, "orb", bit, 1)
-        occ_parts.append(piece)
-
-    inter = None
-    for g in range(GATHER_CHUNKS):
-        part = project(occ_parts[g], orbitals, potentials, g * chunk)
-        inter = part if inter is None else inter + part
+    occ, inter = gather_project(picker, orbitals, potentials)
     scale = weights
     for bit in cell_bits:
         inter = halve(inter, "cell", bit, 1)
@@ -237,7 +309,7 @@
     for r in range(RESPONSE_CHUNKS):
         start = r * width
         part = respond(
-            guesses[r % 2], occ_parts[start // chunk], orbitals, start, start % chunk, width
+            guesses[r % 2], occ, orbitals, start, start, width
         )
         for bit in orders[r % 2]:
             part = halve(part, "orb", bit, 0, jnp.bfloat16)

time: 260 us -> 226 us (0.87)
  waiting for transfers between devices: 112 us -> 63.3 us
  Pallas kernels: 88 us -> 131 us
  starting transfers between devices: 40 us -> 18.2 us
  other arithmetic: 8.39 us -> 4.91 us
    ppermute x30 -> x18, waiting for transfers between devices: 112 us -> 63.3 us  [swap(): return lax.ppermute(x, axis, [(s, s ^ bit) for s in range(n)])]
    pallas_call x2 -> x1, Pallas kernels: 44 us -> 87.1 us  [gather_project(): pl.pallas_call(functools.partial(gather_kernel, bits, chunks, max(1, 256...]
    ppermute x30 -> x18, starting transfers between devices: 40 us -> 18.2 us  [swap(): return lax.ppermute(x, axis, [(s, s ^ bit) for s in range(n)])]
  transfers between devices with their start and end apart: 30 -> 18, of which waited for: 22 -> 13; matrix products, arithmetic and copies ran while one was open for 2% -> 1% of each run, Pallas kernels for 9% -> 0%
where the time goes in v3:
time: 226 us; the launch traced here: 224 us
  Pallas kernels  131 us (58%)
  waiting for transfers between devices  63.3 us (28%)
  starting transfers between devices  18.2 us (8%)
  other arithmetic  4.91 us (2%)
  matrix products  3.3 us (1%)
  local copies, waits for them, and re-layouts  2.38 us (1%)
    pallas_call x1, Pallas kernels, gather_project(): pl.pallas_call(functools.partial(gather_kernel, bits, chunks, max(1, 256...  87.1 us
    ppermute x18, waiting for transfers between devices, swap(): return lax.ppermute(x, axis, [(s, s ^ bit) for s in range(n)])  63.3 us
    pallas_call x4, Pallas kernels, respond(): pl.pallas_call(functools.partial(respond_kernel, max(1, 256 // stored)),...  35.8 us
    ppermute x18, starting transfers between devices, swap(): return lax.ppermute(x, axis, [(s, s ^ bit) for s in range(n)])  18.2 us
    pallas_call x1, Pallas kernels, mix_rows(): pl.pallas_call(mix_kernel, out_shape=jax.ShapeDtypeStruct((held, rows, si...  8.37 us
  transfers between devices with their start and end apart: 18, of which 13 were waited for; matrix products, arithmetic and copies ran while one was open for 1% of the time, Pallas kernels for 0%

profile of v3, /device:TPU:0, one launch (start us, length us, event | category | flops | bytes accessed | tf_op | source)
XLA Modules:
  0.0 223.9 jit_solution(14795706131186051561)
XLA Ops:
  0.0 1.4 compare_convert_fusion.picker
  1.4 87.1 %gather_project.1 = (bf16[64,16384]{1,0:T(8,128)(2,1)}, f32[96,4096]{1,0:T(8,128)}) custom-call(bf16[64,64]{1,0:T(8,128)(2,1)} %compare_convert_fusion.picker, bf16[64,16384]{1,0:T(8,128)(2,1)} %orb_ref.7, bf16[96,16384]{1,0:T(8,128)(2,1)} %pot.1), custom_call_target="tpu_custom_call" | custom-call | tf_op jit(solution)/shard_map/gather_project/pallas_call | solution.py:168
  88.5 1.3 constant_dynamic-slice_fusion.2
  90.0 0.1 fusion.2
  90.1 0.2 select_reduce_fusion
  90.3 1.9 collective-permute-done
  92.2 0.1 dynamic-slice_add_fusion
  92.3 1.6 collective-permute-start.1
  94.1 0.1 divide_multiply_fusion
  94.2 0.1 div.68
  94.3 9.2 %collective-permute-done.1 = f32[96,1024]{1,0:T(8,128)S(1)} collective-permute-done((f32[96,1024]{1,0:T(8,128)S(1)}, f32[96,1024]{1,0:T(8,128)S(1)}, u32[]{:S(2)}, u32[]{:S(2)}) %collective-permute-start.1) | collective-permute-done | bytes 393248 | tf_op jit(solution)/shard_map/ppermute | solution.py:19
  103.6 1.6 collective-permute-start.2
  105.2 4.5 %collective-permute-done.2 = bf16[96,1024]{1,0:T(8,128)(2,1)S(1)} collective-permute-done((bf16[96,1024]{1,0:T(8,128)(2,1)S(1)}, bf16[96,1024]{1,0:T(8,128)(2,1)S(1)}, u32[]{:S(2)}, u32[]{:S(2)}) %collective-permute-start.2) | collective-permute-done | bytes 196640 | tf_op jit(solution)/shard_map/ppermute | solution.py:19
  110.0 1.6 collective-permute-done.3
  111.6 0.1 broadcast_select_fusion.1
  111.8 1.2 fusion.1.guess_ref
  113.0 8.9 %respond.7 = f32[96,4096]{1,0:T(8,128)} custom-call(bf16[96,4096]{1,0:T(8,128)(2,1)} %fusion.1.guess_ref, bf16[64,16384]{1,0:T(8,128)(2,1)} %get-tuple-element.8.occ_ref, bf16[64,16384]{1,0:T(8,128)(2,1)} %orb_ref.7), custom_call_target="tpu_custom_call" | custom-call | flops 9663676416 | bytes 2621440 | tf_op jit(solution)/shard_map/respond/pallas_call | solution.py:210
  121.9 9.0 %respond.5 = f32[96,4096]{1,0:T(8,128)} custom-call(bf16[96,4096]{1,0:T(8,128)(2,1)} %fusion.1.guess_ref, bf16[64,16384]{1,0:T(8,128)(2,1)} %get-tuple-element.8.occ_ref, bf16[64,16384]{1,0:T(8,128)(2,1)} %orb_ref.7), custom_call_target="tpu_custom_call" | custom-call | flops 9663676416 | bytes 2621440 | tf_op jit(solution)/shard_map/respond/pallas_call | solution.py:210
  130.9 1.2 fusion.guess_ref
  132.1 8.9 %respond.6 = f32[96,4096]{1,0:T(8,128)} custom-call(bf16[96,4096]{1,0:T(8,128)(2,1)} %fusion.guess_ref, bf16[64,16384]{1,0:T(8,128)(2,1)} %get-tuple-element.8.occ_ref, bf16[64,16384]{1,0:T(8,128)(2,1)} %orb_ref.7), custom_call_target="tpu_custom_call" | custom-call | flops 9663676416 | bytes 2621440 | tf_op jit(solution)/shard_map/respond/pallas_call | solution.py:210
  141.0 9.0 %respond.4 = f32[96,4096]{1,0:T(8,128)} custom-call(bf16[96,4096]{1,0:T(8,128)(2,1)} %fusion.guess_ref, bf16[64,16384]{1,0:T(8,128)(2,1)} %get-tuple-element.8.occ_ref, bf16[64,16384]{1,0:T(8,128)(2,1)} %orb_ref.7), custom_call_target="tpu_custom_call" | custom-call | flops 9663676416 | bytes 2621440 | tf_op jit(solution)/shard_map/respond/pallas_call | solution.py:210
  150.1 0.7 collective-permute-start.13
  150.8 1.5 collective-permute-start.7
  152.3 1.9 collective-permute-start.10
  154.3 0.2 collective-permute-start.4
  154.5 7.6 %collective-permute-done.13 = bf16[48,4096]{1,0:T(8,128)(2,1)S(1)} collective-permute-done((bf16[48,4096]{1,0:T(8,128)(2,1)S(1)}, bf16[48,4096]{1,0:T(8,128)(2,1)S(1)}, u32[]{:S(2)}, u32[]{:S(2)}) %collective-permute-start.13) | collective-permute-done | bytes 393248 | tf_op jit(solution)/shard_map/ppermute | solution.py:19
  162.2 1.9 collective-permute-start.14
  164.1 9.8 %collective-permute-done.7 = bf16[48,4096]{1,0:T(8,128)(2,1)S(1)} collective-permute-done((bf16[48,4096]{1,0:T(8,128)(2,1)S(1)}, bf16[48,4096]{1,0:T(8,128)(2,1)S(1)}, u32[]{:S(2)}, u32[]{:S(2)}) %collective-permute-start.7) | collective-permute-done | bytes 393248 | tf_op jit(solution)/shard_map/ppermute | solution.py:19
  174.3 2.2 collective-permute-start.11
  176.6 0.1 collective-permute-start.5
  176.8 1.8 collective-permute-start.15
  178.6 5.8 %collective-permute-done.8 = bf16[24,4096]{1,0:T(8,128)(2,1)S(1)} collective-permute-done((bf16[24,4096]{1,0:T(8,128)(2,1)S(1)}, bf16[24,4096]{1,0:T(8,128)(2,1)S(1)}, u32[]{:S(2)}, u32[]{:S(2)}) %collective-permute-start.8) | collective-permute-done | bytes 196640 | tf_op jit(solution)/shard_map/ppermute | solution.py:19
  184.5 1.9 collective-permute-start.9
  186.5 0.3 collective-permute-start.12
  186.8 2.2 collective-permute-done.5
  189.0 0.6 collective-permute-start.6
  189.7 0.3 collective-permute-done.9
  190.1 7.2 %collective-permute-done.12 = bf16[12,4096]{1,0:T(8,128)(2,1)S(1)} collective-permute-done((bf16[12,4096]{1,0:T(8,128)(2,1)S(1)}, bf16[12,4096]{1,0:T(8,128)(2,1)S(1)}, u32[]{:S(2)}, u32[]{:S(2)}) %collective-permute-start.12) | collective-permute-done | bytes 98336 | tf_op jit(solution)/shard_map/ppermute | solution.py:19
  197.3 2.4 %collective-permute-done.6 = bf16[12,4096]{1,0:T(8,128)(2,1)S(1)} collective-permute-done((bf16[12,4096]{1,0:T(8,128)(2,1)S(1)}, bf16[12,4096]{1,0:T(8,128)(2,1)S(1)}, u32[]{:S(2)}, u32[]{:S(2)}) %collective-permute-start.6) | collective-permute-done | bytes 98336 | tf_op jit(solution)/shard_map/ppermute | solution.py:19
  199.9 0.2 reshape.57
  200.1 0.8 convolution_convert_fusion.2
  200.9 1.6 collective-permute-start.16
  202.5 9.3 %collective-permute-done.16 = bf16[12,64,256]{2,1,0:T(8,128)(2,1)S(1)} collective-permute-done((bf16[12,64,256]{2,1,0:T(8,128)(2,1)S(1)}, bf16[12,64,256]{2,1,0:T(8,128)(2,1)S(1)}, u32[]{:S(2)}, u32[]{:S(2)}) %collective-permute-start.16) | collective-permute-done | bytes 393248 | tf_op jit(solution)/shard_map/ppermute | solution.py:19
  212.0 0.1 fusion.5
  212.1 0.7 pad_maximum_fusion.7.mixer_ref
  212.8 1.4 collective-permute-done.17
  214.2 1.3 pad_maximum_fusion.stack_ref
  215.5 8.4 %mix_rows.1 = f32[12,64,256]{2,1,0:T(8,128)} custom-call(f32[64,256]{1,0:T(8,128)} %pad_maximum_fusion.7.mixer_ref, bf16[12,256,256]{2,1,0:T(8,128)(2,1)} %pad_maximum_fusion.stack_ref), custom_call_target="tpu_custom_call" | custom-call | tf_op jit(solution)/shard_map/mix_rows/pallas_call | solution.py:242
  (66 shorter events, 1.9 us)
Async XLA Ops:
  0.0 200.1 %copy-start = (f32[256,256]{1,0:T(8,128)S(1)}, f32[256,256]{1,0:T(8,128)}, u32[]{:S(2)}) copy-start(f32[256,256]{1,0:T(8,128)} %param.13) | copy-start | bytes 786436
  88.5 1.5 copy-start.10
  88.5 1.6 copy-start.9
  88.5 3.7 %copy-start.1 = (f32[96,4096]{1,0:T(8,128)S(1)}, f32[96,4096]{1,0:T(8,128)}, u32[]{:S(2)}) copy-start(f32[96,4096]{1,0:T(8,128)} %get-tuple-element.7) | copy-start | bytes 4718596
  89.8 2.4 %collective-permute-start = (f32[96,2048]{1,0:T(8,128)S(1)}, f32[96,2048]{1,0:T(8,128)S(1)}, u32[]{:S(2)}, u32[]{:S(2)}) collective-permute-start(f32[96,2048]{1,0:T(8,128)S(1)} %constant_dynamic-slice_fusion.2), channel_id=1, source_target_pairs={{0,1},{1,0},{2,3},{3,2},{4,5},{5,4},{6,7},{7,6},{8,9},{9,8},{10,11... | collective-permute-start | bytes 2359304 | tf_op jit(solution)/shard_map/ppermute | solution.py:19
  92.3 11.2 %collective-permute-start.1 = (f32[96,1024]{1,0:T(8,128)S(1)}, f32[96,1024]{1,0:T(8,128)S(1)}, u32[]{:S(2)}, u32[]{:S(2)}) collective-permute-start(f32[96,1024]{1,0:T(8,128)S(1)} %constant_dynamic-slice_fusion.1), channel_id=1, source_target_pairs={{0,2},{1,3},{2,0},{3,1},{4,6},{5,7},{6,4},{7,5},{8,10},{9,11},{10,... | collective-permute-start | bytes 1179656 | tf_op jit(solution)/shard_map/ppermute | solution.py:19
  103.6 6.2 %collective-permute-start.2 = (bf16[96,1024]{1,0:T(8,128)(2,1)S(1)}, bf16[96,1024]{1,0:T(8,128)(2,1)S(1)}, u32[]{:S(2)}, u32[]{:S(2)}) collective-permute-start(bf16[96,1024]{1,0:T(8,128)(2,1)S(1)} %multiply_convert_fusion), channel_id=1, source_target_pairs={{0,2},{1,3},{2,0},{3,1},{4,6},{5,7},{6,4},{7,5},{8,10},{9,11},{10,... | collective-permute-start | bytes 589832 | tf_op jit(solution)/shard_map/ppermute | solution.py:19
  105.2 6.6 %copy-start.8 = (bf16[96,96]{1,0:T(8,128)(2,1)S(1)}, bf16[96,96]{1,0:T(8,128)(2,1)}, u32[]{:S(2)}) copy-start(bf16[96,96]{1,0:T(8,128)(2,1)} %constant.223.clone) | copy-start | bytes 55300
  109.8 1.8 collective-permute-start.3
  121.9 9.0 %copy-start.7 = (bf16[96,96]{1,0:T(8,128)(2,1)S(1)}, bf16[96,96]{1,0:T(8,128)(2,1)}, u32[]{:S(2)}) copy-start(bf16[96,96]{1,0:T(8,128)(2,1)} %constant.222.clone) | copy-start | bytes 55300
  141.0 9.0 %copy-start.5 = (f32[96,4096]{1,0:T(8,128)S(1)}, f32[96,4096]{1,0:T(8,128)}, u32[]{:S(2)}) copy-start(f32[96,4096]{1,0:T(8,128)} %respond.7) | copy-start | bytes 4718596
  141.0 9.7 %copy-start.4 = (f32[96,4096]{1,0:T(8,128)S(1)}, f32[96,4096]{1,0:T(8,128)}, u32[]{:S(2)}) copy-start(f32[96,4096]{1,0:T(8,128)} %respond.5) | copy-start | bytes 4718596
  141.0 11.3 %copy-start.3 = (f32[96,4096]{1,0:T(8,128)S(1)}, f32[96,4096]{1,0:T(8,128)}, u32[]{:S(2)}) copy-start(f32[96,4096]{1,0:T(8,128)} %respond.6) | copy-start | bytes 4718596
  150.0 4.2 %copy-start.2 = (f32[96,4096]{1,0:T(8,128)S(1)}, f32[96,4096]{1,0:T(8,128)}, u32[]{:S(2)}) copy-start(f32[96,4096]{1,0:T(8,128)} %respond.4) | copy-start | bytes 4718596
  150.1 12.1 %collective-permute-start.13 = (bf16[48,4096]{1,0:T(8,128)(2,1)S(1)}, bf16[48,4096]{1,0:T(8,128)(2,1)S(1)}, u32[]{:S(2)}, u32[]{:S(2)}) collective-permute-start(bf16[48,4096]{1,0:T(8,128)(2,1)S(1)} %dynamic-slice_convert_fusion), channel_id=1, source_target_pairs={{0,8},{4,12},{8,0},{12,4},{16,24},{20,28},{24,16},{28,20},{1,9},{5... | collective-permute-start | bytes 1179656 | tf_op jit(solution)/shard_map/ppermute | solution.py:19
  150.8 23.1 %collective-permute-start.7 = (bf16[48,4096]{1,0:T(8,128)(2,1)S(1)}, bf16[48,4096]{1,0:T(8,128)(2,1)S(1)}, u32[]{:S(2)}, u32[]{:S(2)}) collective-permute-start(bf16[48,4096]{1,0:T(8,128)(2,1)S(1)} %dynamic-slice_convert_fusion.2), channel_id=1, source_target_pairs={{0,8},{4,12},{8,0},{12,4},{16,24},{20,28},{24,16},{28,20},{1,9},{5... | collective-permute-start | bytes 1179656 | tf_op jit(solution)/shard_map/ppermute | solution.py:19
  152.3 21.8 %collective-permute-start.10 = (bf16[48,4096]{1,0:T(8,128)(2,1)S(1)}, bf16[48,4096]{1,0:T(8,128)(2,1)S(1)}, u32[]{:S(2)}, u32[]{:S(2)}) collective-permute-start(bf16[48,4096]{1,0:T(8,128)(2,1)S(1)} %dynamic-slice_convert_fusion.1), channel_id=1, source_target_pairs={{0,4},{4,0},{8,12},{12,8},{16,20},{20,16},{24,28},{28,24},{1,5},{5... | collective-permute-start | bytes 1179656 | tf_op jit(solution)/shard_map/ppermute | solution.py:19
  154.3 22.1 %collective-permute-start.4 = (bf16[48,4096]{1,0:T(8,128)(2,1)S(1)}, bf16[48,4096]{1,0:T(8,128)(2,1)S(1)}, u32[]{:S(2)}, u32[]{:S(2)}) collective-permute-start(bf16[48,4096]{1,0:T(8,128)(2,1)S(1)} %dynamic-slice_convert_fusion.3), channel_id=1, source_target_pairs={{0,4},{4,0},{8,12},{12,8},{16,20},{20,16},{24,28},{28,24},{1,5},{5... | collective-permute-start | bytes 1179656 | tf_op jit(solution)/shard_map/ppermute | solution.py:19
  162.2 14.4 %collective-permute-start.14 = (bf16[24,4096]{1,0:T(8,128)(2,1)S(1)}, bf16[24,4096]{1,0:T(8,128)(2,1)S(1)}, u32[]{:S(2)}, u32[]{:S(2)}) collective-permute-start(bf16[24,4096]{1,0:T(8,128)(2,1)S(1)} %dynamic-slice_convert_fusion.4), channel_id=1, source_target_pairs={{0,16},{4,20},{8,24},{12,28},{16,0},{20,4},{24,8},{28,12},{1,17},{... | collective-permute-start | bytes 589832 | tf_op jit(solution)/shard_map/ppermute | solution.py:19
  174.1 10.3 %collective-permute-start.8 = (bf16[24,4096]{1,0:T(8,128)(2,1)S(1)}, bf16[24,4096]{1,0:T(8,128)(2,1)S(1)}, u32[]{:S(2)}, u32[]{:S(2)}) collective-permute-start(bf16[24,4096]{1,0:T(8,128)(2,1)S(1)} %dynamic-slice_convert_fusion.6), channel_id=1, source_target_pairs={{0,16},{4,20},{8,24},{12,28},{16,0},{20,4},{24,8},{28,12},{1,17},{... | collective-permute-start | bytes 589832 | tf_op jit(solution)/shard_map/ppermute | solution.py:19
  174.3 12.2 %collective-permute-start.11 = (bf16[24,4096]{1,0:T(8,128)(2,1)S(1)}, bf16[24,4096]{1,0:T(8,128)(2,1)S(1)}, u32[]{:S(2)}, u32[]{:S(2)}) collective-permute-start(bf16[24,4096]{1,0:T(8,128)(2,1)S(1)} %dynamic-slice_convert_fusion.5), channel_id=1, source_target_pairs={{0,8},{4,12},{8,0},{12,4},{16,24},{20,28},{24,16},{28,20},{1,9},{5... | collective-permute-start | bytes 589832 | tf_op jit(solution)/shard_map/ppermute | solution.py:19
  176.6 12.4 %collective-permute-start.5 = (bf16[24,4096]{1,0:T(8,128)(2,1)S(1)}, bf16[24,4096]{1,0:T(8,128)(2,1)S(1)}, u32[]{:S(2)}, u32[]{:S(2)}) collective-permute-start(bf16[24,4096]{1,0:T(8,128)(2,1)S(1)} %dynamic-slice_convert_fusion.7), channel_id=1, source_target_pairs={{0,8},{4,12},{8,0},{12,4},{16,24},{20,28},{24,16},{28,20},{1,9},{5... | collective-permute-start | bytes 589832 | tf_op jit(solution)/shard_map/ppermute | solution.py:19
  176.8 12.9 %collective-permute-start.15 = (bf16[12,4096]{1,0:T(8,128)(2,1)S(1)}, bf16[12,4096]{1,0:T(8,128)(2,1)S(1)}, u32[]{:S(2)}, u32[]{:S(2)}) collective-permute-start(bf16[12,4096]{1,0:T(8,128)(2,1)S(1)} %dynamic-slice_convert_fusion.8), channel_id=1, source_target_pairs={{0,4},{4,0},{8,12},{12,8},{16,20},{20,16},{24,28},{28,24},{1,5},{5... | collective-permute-start | bytes 294920 | tf_op jit(solution)/shard_map/ppermute | solution.py:19
  184.5 5.5 %collective-permute-start.9 = (bf16[12,4096]{1,0:T(8,128)(2,1)S(1)}, bf16[12,4096]{1,0:T(8,128)(2,1)S(1)}, u32[]{:S(2)}, u32[]{:S(2)}) collective-permute-start(bf16[12,4096]{1,0:T(8,128)(2,1)S(1)} %dynamic-slice_convert_fusion.10), channel_id=1, source_target_pairs={{0,4},{4,0},{8,12},{12,8},{16,20},{20,16},{24,28},{28,24},{1,5},{5... | collective-permute-start | bytes 294920 | tf_op jit(solution)/shard_map/ppermute | solution.py:19
  186.5 10.8 %collective-permute-start.12 = (bf16[12,4096]{1,0:T(8,128)(2,1)S(1)}, bf16[12,4096]{1,0:T(8,128)(2,1)S(1)}, u32[]{:S(2)}, u32[]{:S(2)}) collective-permute-start(bf16[12,4096]{1,0:T(8,128)(2,1)S(1)} %dynamic-slice_convert_fusion.9), channel_id=1, source_target_pairs={{0,16},{4,20},{8,24},{12,28},{16,0},{20,4},{24,8},{28,12},{1,17},{... | collective-permute-start | bytes 294920 | tf_op jit(solution)/shard_map/ppermute | solution.py:19
  189.0 10.7 %collective-permute-start.6 = (bf16[12,4096]{1,0:T(8,128)(2,1)S(1)}, bf16[12,4096]{1,0:T(8,128)(2,1)S(1)}, u32[]{:S(2)}, u32[]{:S(2)}) collective-permute-start(bf16[12,4096]{1,0:T(8,128)(2,1)S(1)} %dynamic-slice_convert_fusion.11), channel_id=1, source_target_pairs={{0,16},{4,20},{8,24},{12,28},{16,0},{20,4},{24,8},{28,12},{1,17},{... | collective-permute-start | bytes 294920 | tf_op jit(solution)/shard_map/ppermute | solution.py:19
  200.1 11.9 %copy-start.6 = (f32[256,256]{1,0:T(8,128)S(1)}, f32[256,256]{1,0:T(8,128)}, u32[]{:S(2)}) copy-start(f32[256,256]{1,0:T(8,128)} %param.12) | copy-start | bytes 786436
  200.9 10.9 %collective-permute-start.16 = (bf16[12,64,256]{2,1,0:T(8,128)(2,1)S(1)}, bf16[12,64,256]{2,1,0:T(8,128)(2,1)S(1)}, u32[]{:S(2)}, u32[]{:S(2)}) collective-permute-start(bf16[12,64,256]{2,1,0:T(8,128)(2,1)S(1)} %bitcast.10), channel_id=1, source_target_pairs={{0,2},{1,3},{2,0},{3,1},{4,6},{5,7},{6,4},{7,5},{8,10},{9,11},{10,... | collective-permute-start | bytes 1179656 | tf_op jit(solution)/shard_map/ppermute | solution.py:19
  211.9 2.4 %collective-permute-start.17 = (bf16[12,128,256]{2,1,0:T(8,128)(2,1)S(1)}, bf16[12,128,256]{2,1,0:T(8,128)(2,1)S(1)}, u32[]{:S(2)}, u32[]{:S(2)}) collective-permute-start(bf16[12,128,256]{2,1,0:T(8,128)(2,1)S(1)} %pad_maximum_fusion.3), channel_id=1, source_target_pairs={{0,1},{1,0},{2,3},{3,2},{4,5},{5,4},{6,7},{7,6},{8,9},{9,8},{10,11... | collective-permute-start | bytes 2359304 | tf_op jit(solution)/shard_map/ppermute | solution.py:19

commit v4 on v3

--- a/solution.py
+++ b/solution.py
@@ -10,7 +10,6 @@
 
 SIDE = 256
 MESH = pl.DeviceIdType.MESH
-RESPONSE_CHUNKS = 4
 VMEM = 56 * 1024 * 1024
 
 
@@ -42,10 +41,6 @@
 def bits_of(axis):
     n = lax.axis_size(axis)
     return [1 << k for k in range(n.bit_length() - 1)]
-
-
-def pair_rows(occ_ref, orb, first, count):
-    return jnp.concatenate([occ_ref[i : i + 1, :] * orb for i in range(first, first + count)], 0)
 
 
 def partner_of(axis, bit):
@@ -187,44 +182,98 @@
     )(picker, orbitals, potentials)
 
 
-def respond_kernel(group, guess_ref, occ_ref, orb_ref, out_ref):
-    orb = orb_ref[...]
-    rows = group * orb.shape[0]
-    total = None
-    for k in range(occ_ref.shape[0] // group):
-        pairs = pair_rows(occ_ref, orb, k * group, group)
-        term = jnp.dot(
-            guess_ref[:, k * rows : (k + 1) * rows], pairs, preferred_element_type=jnp.float32
-        )
-        total = term if total is None else total + term
-    out_ref[...] = total
-
-
-def respond(guess, occ, orbitals, start, occ_start, width):
-    slots = occ.shape[0]
+def respond_kernel(bits, chunks, group, *refs):
+    depth = len(bits)
+    guess_refs, (occ, orb, out), rest = refs[:2], refs[2:5], refs[5:]
+    keeps, sends, lands = rest[:depth], rest[depth : 2 * depth], rest[2 * depth : 3 * depth]
+    sent, came = rest[3 * depth :]
+    points = orb.shape[1]
+    chunk = points // chunks
+    block = min(512, chunk)
+    orders = [bits, bits[1:] + bits[:1]]
+    flying = [None] * chunks
+
+    def split(value, bit, step, span):
+        half = value.shape[0] // 2
+        low, high = value[:half], value[half:]
+        at_low = upper("orb", bit) == 0
+        keeps[step][:, span] = jnp.where(at_low, low, high)
+        sends[step][:, span] = jnp.where(at_low, high, low).astype(sends[step].dtype)
+
+    def push(c, step):
+        span = pl.ds(c * chunk, chunk)
+        copy = pltpu.make_async_remote_copy(
+            src_ref=sends[step].at[:, span],
+            dst_ref=lands[step].at[:, span],
+            send_sem=sent.at[c, step],
+            recv_sem=came.at[c, step],
+            device_id={"orb": partner_of("orb", orders[c % 2][step])},
+            device_id_type=MESH,
+        )
+        copy.start()
+        flying[c] = copy
+
+    def compute(c):
+        guess = guess_refs[c % 2]
+
+        @pl.loop(0, chunk // block)
+        def _(b):
+            span = pl.ds(pl.multiple_of(c * chunk + b * block, block), block)
+            basis = orb[:, span]
+            rows = group * basis.shape[0]
+            total = None
+            for k in range(occ.shape[0] // group):
+                pairs = jnp.concatenate(
+                    [occ[i : i + 1, span] * basis for i in range(k * group, (k + 1) * group)], 0
+                )
+                term = jnp.dot(
+                    guess[:, k * rows : (k + 1) * rows], pairs, preferred_element_type=jnp.float32
+                )
+                total = term if total is None else total + term
+            split(total, orders[c % 2][0], 0, span)
+
+    def advance(c, step):
+        flying[c].wait()
+        span = pl.ds(c * chunk, chunk)
+        value = keeps[step - 1][:, span] + lands[step - 1][:, span].astype(jnp.float32)
+        if step == depth:
+            out[:, span] = value
+        else:
+            split(value, orders[c % 2][step], step, span)
+            push(c, step)
+
+    greet("orb", bits)
+    lag = 2
+    for tick in range(chunks + lag * depth):
+        if tick < chunks:
+            compute(tick)
+            push(tick, 0)
+        for step in range(1, depth + 1):
+            c = tick - lag * step
+            if 0 <= c < chunks:
+                advance(c, step)
+
+
+def respond(guesses, occ, orbitals):
+    _, points = occ.shape
     stored = orbitals.shape[0]
-    nv, pairs = guess.shape
-    block = min(512, width)
-    shift = start // block
-    occ_shift = occ_start // block
+    nv, _ = guesses[0].shape
+    bits = bits_of("orb")
+    chunks = max(1, min(16, points // 512))
+    sizes = [nv >> (k + 1) for k in range(len(bits))]
     return pl.pallas_call(
-        functools.partial(respond_kernel, max(1, 256 // stored)),
-        out_shape=jax.ShapeDtypeStruct((nv, width), jnp.float32),
-        grid=(width // block,),
-        in_specs=[
-            pl.BlockSpec((nv, pairs), lambda s: (0, 0)),
-            pl.BlockSpec((slots, block), lambda s: (0, s + occ_shift)),
-            pl.BlockSpec((stored, block), lambda s: (0, s + shift)),
-        ],
-        out_specs=pl.BlockSpec((nv, block), lambda s: (0, s)),
-        compiler_params=pltpu.CompilerParams(vmem_limit_bytes=VMEM),
-        cost_estimate=pl.CostEstimate(
-            flops=2 * pairs * nv * width * 3,
-            bytes_accessed=2 * width * (slots + stored) + 4 * nv * width,
-            transcendentals=0,
+        functools.partial(respond_kernel, bits, chunks, max(1, 256 // stored)),
+        out_shape=jax.ShapeDtypeStruct((nv >> len(bits), points), jnp.float32),
+        in_specs=[pl.BlockSpec(memory_space=pltpu.VMEM)] * 4,
+        out_specs=pl.BlockSpec(memory_space=pltpu.VMEM),
+        scratch_shapes=[pltpu.VMEM((n, points), jnp.float32) for n in sizes]
+        + [pltpu.VMEM((n, points), jnp.bfloat16) for n in sizes] * 2
+        + [pltpu.SemaphoreType.DMA((chunks, len(bits)))] * 2,
+        compiler_params=pltpu.CompilerParams(
+            vmem_limit_bytes=VMEM, collective_id=1, has_side_effects=True
         ),
         name="respond",
-    )(guess, occ, orbitals)
+    )(*guesses, occ, orbitals)
 
 
 def mix_kernel(mixer_ref, stack_ref, out_ref):
@@ -297,7 +346,6 @@
     for bit in cell_bits[::-1]:
         guess = double(guess, "cell", bit, 1)
 
-    width = points_dev // RESPONSE_CHUNKS
     guesses = []
     for order in orders:
         rows = owner_order(nv, orb_count, order)
@@ -305,16 +353,7 @@
         guesses.append(
             jnp.dot(place, guess, preferred_element_type=jnp.float32).astype(jnp.bfloat16)
         )
-    owned = []
-    for r in range(RESPONSE_CHUNKS):
-        start = r * width
-        part = respond(
-            guesses[r % 2], occ, orbitals, start, start, width
-        )
-        for bit in orders[r % 2]:
-            part = halve(part, "orb", bit, 0, jnp.bfloat16)
-        owned.append(part)
-    owned_sum = jnp.concatenate(owned, 1)
+    owned_sum = respond(guesses, occ, orbitals)
 
     row_count = points_dev // SIDE
     held = owned_sum.shape[0]

time: 226 us -> 192 us (0.85)
  waiting for transfers between devices: 63.3 us -> 25.5 us
  Pallas kernels: 131 us -> 151 us
  starting transfers between devices: 18.2 us -> 4.95 us
    ppermute x18 -> x6, waiting for transfers between devices: 63.3 us -> 25.5 us  [swap(): return lax.ppermute(x, axis, [(s, s ^ bit) for s in range(n)])]
    pallas_call x4 -> x1, Pallas kernels: 35.8 us -> 55 us  [respond(): pl.pallas_call(functools.partial(respond_kernel, bits, chunks, max(1, 256...]
    ppermute x18 -> x6, starting transfers between devices: 18.2 us -> 4.95 us  [swap(): return lax.ppermute(x, axis, [(s, s ^ bit) for s in range(n)])]
  transfers between devices with their start and end apart: 18 -> 6, of which waited for: 13 -> 6; matrix products, arithmetic and copies ran while one was open for 1% -> 1% of each run, Pallas kernels for 0% -> 0%
where the time goes in v4:
time: 192 us
  Pallas kernels  151 us (79%)
  waiting for transfers between devices  25.5 us (13%)
  starting transfers between devices  4.95 us (3%)
  other arithmetic  4.2 us (2%)
  matrix products  3.31 us (2%)
  local copies, waits for them, and re-layouts  3.18 us (2%)
    pallas_call x1, Pallas kernels, gather_project(): pl.pallas_call(functools.partial(gather_kernel, bits, chunks, max(1, 256...  87.1 us
    pallas_call x1, Pallas kernels, respond(): pl.pallas_call(functools.partial(respond_kernel, bits, chunks, max(1, 256...  55 us
    ppermute x6, waiting for transfers between devices, swap(): return lax.ppermute(x, axis, [(s, s ^ bit) for s in range(n)])  25.5 us
    pallas_call x1, Pallas kernels, mix_rows(): pl.pallas_call(mix_kernel, out_shape=jax.ShapeDtypeStruct((held, rows, si...  8.37 us
    ppermute x6, starting transfers between devices, swap(): return lax.ppermute(x, axis, [(s, s ^ bit) for s in range(n)])  4.95 us
  transfers between devices with their start and end apart: 6, of which 6 were waited for; matrix products, arithmetic and copies ran while one was open for 1% of the time, Pallas kernels for 0%

profile of v4, /device:TPU:0, one launch (start us, length us, event | category | flops | bytes accessed | tf_op | source)
XLA Modules:
  0.0 192.0 jit_solution(12404681401859472203)
XLA Ops:
  0.0 0.0 copy-start
  0.0 1.4 compare_convert_fusion.picker
  1.4 87.1 %gather_project.1 = (bf16[64,16384]{1,0:T(8,128)(2,1)}, f32[96,4096]{1,0:T(8,128)}) custom-call(bf16[64,64]{1,0:T(8,128)(2,1)} %compare_convert_fusion.picker, bf16[64,16384]{1,0:T(8,128)(2,1)} %refs_3_.1, bf16[96,16384]{1,0:T(8,128)(2,1)} %pot.1), custom_call_target="tpu_custom_call" | custom-call | tf_op jit(solution)/shard_map/gather_project/pallas_call | solution.py:163
  88.5 0.0 copy-start.6
  88.5 0.0 copy-start.5
  88.5 0.0 copy-start.1
  88.5 1.3 constant_dynamic-slice_fusion.2
  89.9 0.1 collective-permute-start
  90.0 0.0 copy-done.6
  90.0 0.1 fusion.2
  90.1 0.0 copy-done.5
  90.1 0.2 select_reduce_fusion
  90.3 1.9 collective-permute-done
  92.2 0.0 copy-done.1
  92.2 0.1 dynamic-slice_add_fusion
  92.3 1.6 collective-permute-start.1
  94.0 0.1 dynamic-slice_multiply_fusion
  94.0 0.1 dynamic_slice.47
  94.1 0.1 divide_multiply_fusion
  94.2 0.1 div.44
  94.3 0.1 constant_dynamic-slice_fusion
  94.4 9.2 %collective-permute-done.1 = f32[96,1024]{1,0:T(8,128)S(1)} collective-permute-done((f32[96,1024]{1,0:T(8,128)S(1)}, f32[96,1024]{1,0:T(8,128)S(1)}, u32[]{:S(2)}, u32[]{:S(2)}) %collective-permute-start.1) | collective-permute-done | bytes 393248 | tf_op jit(solution)/shard_map/ppermute | solution.py:18
  103.6 0.1 multiply_convert_fusion
  103.6 1.6 collective-permute-start.2
  105.2 4.5 %collective-permute-done.2 = bf16[96,1024]{1,0:T(8,128)(2,1)S(1)} collective-permute-done((bf16[96,1024]{1,0:T(8,128)(2,1)S(1)}, bf16[96,1024]{1,0:T(8,128)(2,1)S(1)}, u32[]{:S(2)}, u32[]{:S(2)}) %collective-permute-start.2) | collective-permute-done | bytes 196640 | tf_op jit(solution)/shard_map/ppermute | solution.py:18
  109.8 0.1 collective-permute-start.3
  109.9 0.0 copy-start.3
  109.9 1.7 collective-permute-done.3
  111.6 0.1 broadcast_select_fusion.1
  111.8 0.0 copy-done.4
  111.8 1.3 fusion.1.refs_1_
  113.1 0.0 copy-done.3
  113.1 1.2 fusion.refs_0_
  114.3 55.0 %respond.1 = f32[12,16384]{1,0:T(8,128)} custom-call(bf16[96,4096]{1,0:T(8,128)(2,1)} %fusion.refs_0_, bf16[96,4096]{1,0:T(8,128)(2,1)} %fusion.1.refs_1_, bf16[64,16384]{1,0:T(8,128)(2,1)} %get-tuple-element.8.refs_2_, bf16[64,16384]{1,0:T(8,128)(2,1)} %refs_3_.1), custom_call_target="tpu_custom_call" | custom-call | tf_op jit(solution)/shard_map/respond/pallas_call | solution.py:264
  169.3 1.4 reshape.57
  170.8 0.0 copy-done
  170.8 0.0 copy-start.2
  170.8 0.8 convolution_convert_fusion.2
  171.6 1.5 collective-permute-start.4
  173.2 6.8 %collective-permute-done.4 = bf16[12,64,256]{2,1,0:T(8,128)(2,1)S(1)} collective-permute-done((bf16[12,64,256]{2,1,0:T(8,128)(2,1)S(1)}, bf16[12,64,256]{2,1,0:T(8,128)(2,1)S(1)}, u32[]{:S(2)}, u32[]{:S(2)}) %collective-permute-start.4) | collective-permute-done | bytes 393248 | tf_op jit(solution)/shard_map/ppermute | solution.py:18
  180.0 0.1 pad_maximum_fusion.2
  180.0 0.1 collective-permute-start.5
  180.1 0.0 copy-done.2
  180.1 0.1 fusion.5
  180.3 0.7 pad_maximum_fusion.6.mixer_ref
  181.0 1.4 collective-permute-done.5
  182.4 1.3 pad_maximum_fusion.stack_ref
  183.6 8.4 %mix_rows.1 = f32[12,64,256]{2,1,0:T(8,128)} custom-call(f32[64,256]{1,0:T(8,128)} %pad_maximum_fusion.6.mixer_ref, bf16[12,256,256]{2,1,0:T(8,128)(2,1)} %pad_maximum_fusion.stack_ref), custom_call_target="tpu_custom_call" | custom-call | tf_op jit(solution)/shard_map/mix_rows/pallas_call | solution.py:291
  (6 shorter events, 0.1 us)
Async XLA Ops:
  0.0 170.8 %copy-start = (f32[256,256]{1,0:T(8,128)S(1)}, f32[256,256]{1,0:T(8,128)}, u32[]{:S(2)}) copy-start(f32[256,256]{1,0:T(8,128)} %param.13) | copy-start | bytes 786436
  88.5 1.5 copy-start.6
  88.5 1.6 copy-start.5
  88.5 3.7 %copy-start.1 = (f32[96,4096]{1,0:T(8,128)S(1)}, f32[96,4096]{1,0:T(8,128)}, u32[]{:S(2)}) copy-start(f32[96,4096]{1,0:T(8,128)} %get-tuple-element.7) | copy-start | bytes 4718596
  89.9 2.4 %collective-permute-start = (f32[96,2048]{1,0:T(8,128)S(1)}, f32[96,2048]{1,0:T(8,128)S(1)}, u32[]{:S(2)}, u32[]{:S(2)}) collective-permute-start(f32[96,2048]{1,0:T(8,128)S(1)} %constant_dynamic-slice_fusion.2), channel_id=1, source_target_pairs={{0,1},{1,0},{2,3},{3,2},{4,5},{5,4},{6,7},{7,6},{8,9},{9,8},{10,11... | collective-permute-start | bytes 2359304 | tf_op jit(solution)/shard_map/ppermute | solution.py:18
  92.3 11.2 %collective-permute-start.1 = (f32[96,1024]{1,0:T(8,128)S(1)}, f32[96,1024]{1,0:T(8,128)S(1)}, u32[]{:S(2)}, u32[]{:S(2)}) collective-permute-start(f32[96,1024]{1,0:T(8,128)S(1)} %constant_dynamic-slice_fusion.1), channel_id=1, source_target_pairs={{0,2},{1,3},{2,0},{3,1},{4,6},{5,7},{6,4},{7,5},{8,10},{9,11},{10,... | collective-permute-start | bytes 1179656 | tf_op jit(solution)/shard_map/ppermute | solution.py:18
  103.6 6.2 %collective-permute-start.2 = (bf16[96,1024]{1,0:T(8,128)(2,1)S(1)}, bf16[96,1024]{1,0:T(8,128)(2,1)S(1)}, u32[]{:S(2)}, u32[]{:S(2)}) collective-permute-start(bf16[96,1024]{1,0:T(8,128)(2,1)S(1)} %multiply_convert_fusion), channel_id=1, source_target_pairs={{0,2},{1,3},{2,0},{3,1},{4,6},{5,7},{6,4},{7,5},{8,10},{9,11},{10,... | collective-permute-start | bytes 589832 | tf_op jit(solution)/shard_map/ppermute | solution.py:18
  105.2 6.6 %copy-start.4 = (bf16[96,96]{1,0:T(8,128)(2,1)S(1)}, bf16[96,96]{1,0:T(8,128)(2,1)}, u32[]{:S(2)}) copy-start(bf16[96,96]{1,0:T(8,128)(2,1)} %constant.144.clone) | copy-start | bytes 55300
  109.8 1.8 collective-permute-start.3
  109.9 3.1 %copy-start.3 = (bf16[96,96]{1,0:T(8,128)(2,1)S(1)}, bf16[96,96]{1,0:T(8,128)(2,1)}, u32[]{:S(2)}) copy-start(bf16[96,96]{1,0:T(8,128)(2,1)} %constant.143.clone) | copy-start | bytes 55300
  170.8 9.3 %copy-start.2 = (f32[256,256]{1,0:T(8,128)S(1)}, f32[256,256]{1,0:T(8,128)}, u32[]{:S(2)}) copy-start(f32[256,256]{1,0:T(8,128)} %param.12) | copy-start | bytes 786436
  171.6 8.3 %collective-permute-start.4 = (bf16[12,64,256]{2,1,0:T(8,128)(2,1)S(1)}, bf16[12,64,256]{2,1,0:T(8,128)(2,1)S(1)}, u32[]{:S(2)}, u32[]{:S(2)}) collective-permute-start(bf16[12,64,256]{2,1,0:T(8,128)(2,1)S(1)} %bitcast.10), channel_id=1, source_target_pairs={{0,2},{1,3},{2,0},{3,1},{4,6},{5,7},{6,4},{7,5},{8,10},{9,11},{10,... | collective-permute-start | bytes 1179656 | tf_op jit(solution)/shard_map/ppermute | solution.py:18
  180.0 2.4 %collective-permute-start.5 = (bf16[12,128,256]{2,1,0:T(8,128)(2,1)S(1)}, bf16[12,128,256]{2,1,0:T(8,128)(2,1)S(1)}, u32[]{:S(2)}, u32[]{:S(2)}) collective-permute-start(bf16[12,128,256]{2,1,0:T(8,128)(2,1)S(1)} %pad_maximum_fusion.2), channel_id=1, source_target_pairs={{0,1},{1,0},{2,3},{3,2},{4,5},{5,4},{6,7},{7,6},{8,9},{9,8},{10,11... | collective-permute-start | bytes 2359304 | tf_op jit(solution)/shard_map/ppermute | solution.py:18
